TPU v7x, 512 devices: a whole 4x4x16 slice. The times are simulated.
512 devices in a mesh: test: 8 (over z_lo, core), bx: 4 (over y), by: 16 (over z_hi, x).
Axes of the slice: x: 4, y: 4, z: 16 (z_hi: 4, z_lo: 4; z = z_hi * 4 + z_lo), core: 2. Of those that a mesh axis runs over, the one named last changes fastest.
Arguments:
- log_conductivity: float32 [32, 128, 256], P('bx', 'by'), may hold values from -3 to 3
- storage: float32 [32, 128, 256], P('bx', 'by'), may hold values from 0.5 to 2
- recharge: float32 [32, 128, 256], P('bx', 'by'), may hold values from -6 to 6
- pump_rate: float32 [32], P('test'), may hold values from 4 to 16
- pump_well: int32 [32], P('test'), may hold values from 0 to 2047
- observed: float32 [32, 2048], P('test'), may hold values from -9 to 9
- owner: int32 [2048], replicated, may hold values from 0 to 63, as said below
- screen_column: int32 [2048], replicated, may hold values from 0 to 63
- screen_top: int32 [2048], replicated, may hold values from 0 to 248
Outputs:
- gradient: float32 [32, 128, 256], P('bx', 'by', 'test')
Inputs may be any that keep to these rules, and one draw needn't show every extreme that they name: `owner`: each brick owns exactly 32 wells.
All inputs are finite; a program needn't handle non-finite values.
Results may differ from a plain program's by a relative error of at most 0.0001.
Values sent between devices are 32-bit elements; how exact they have to be, the bound alone decides.
A program may use at most 64 MiB of HBM per device.

v0:
```python
import jax
import jax.numpy as jnp
from jax import lax
from jax.sharding import PartitionSpec as P

SWEEPS = 3
SCREEN = 8


epsilon = 1e-06


def with_halo(block, sides, width):
    for axis, dim in sides:
        count = lax.axis_size(axis)
        forward = [(i, i + 1) for i in range(count - 1)]
        backward = [(target, source) for source, target in forward]
        low = lax.ppermute(
            lax.slice_in_dim(block, block.shape[dim] - width, None, axis=dim), axis, forward
        )
        high = lax.ppermute(lax.slice_in_dim(block, 0, width, axis=dim), axis, backward)
        block = jnp.concatenate([low, block, high], axis=dim)
    return block


def pad_depth(values):
    return jnp.pad(values, [(0, 0)] * (values.ndim - 1) + [(1, 1)])


def neighbours(padded, centre):
    z_padded = pad_depth(centre)
    return [
        padded[..., 2:, 1:-1, :],
        padded[..., :-2, 1:-1, :],
        padded[..., 1:-1, 2:, :],
        padded[..., 1:-1, :-2, :],
        z_padded[..., 2:],
        z_padded[..., :-2],
    ]


def weighted(conductance, others):
    accumulated = conductance[0] * others[0]
    for position in range(1, 6):
        accumulated = accumulated + conductance[position] * others[position]
    return accumulated


def sensitivity(conductance, heads_field, heads_padded, adjoint_field, adjoint_padded):
    near_heads = neighbours(heads_padded, heads_field)
    near_adjoint = neighbours(adjoint_padded, adjoint_field)
    accumulated = jnp.zeros_like(heads_field)
    for position in range(6):
        accumulated = accumulated + conductance[position] * (heads_field - near_heads[position]) * (
            adjoint_field - near_adjoint[position]
        )
    return -0.5 * accumulated


def relax_field(source, conductance, diagonal):
    iterate = source / diagonal
    for sweep_index in range(SWEEPS - 1):
        padded = with_halo(iterate, (("bx", 1), ("by", 2)), 1)
        iterate = (source + weighted(conductance, neighbours(padded, iterate))) / diagonal
    return iterate


def per_sweep_terms(
    log_conductivity,
    storage,
    recharge,
    pump_rate,
    pump_well,
    observed,
    owner,
    screen_column,
    screen_top,
):
    size_x, size_y, size_z = log_conductivity.shape
    tests_here = pump_rate.shape[0]
    cell_count = size_x * size_y * size_z
    padded_log = with_halo(log_conductivity, (("bx", 0), ("by", 1)), 1)
    conductance = [
        jnp.exp(0.5 * (log_conductivity + other))
        for other in neighbours(padded_log, log_conductivity)
    ]
    diagonal = storage + weighted(conductance, [1.0] * 6)
    brick_index = lax.axis_index("bx") * lax.axis_size("by") + lax.axis_index("by")
    offsets = jnp.arange(SCREEN, dtype=jnp.int32)
    screen_cells = (screen_column * size_z + screen_top)[:, None] + offsets[None, :]
    owned_here = owner == brick_index
    pump_cells = screen_cells[pump_well]
    pump_value = jnp.where(owner[pump_well] == brick_index, -pump_rate, 0.0)
    test_rows = jnp.arange(tests_here, dtype=jnp.int32)[:, None]
    flat_source = jnp.broadcast_to(recharge.reshape(1, cell_count), (tests_here, cell_count))
    flat_source = flat_source.at[test_rows, pump_cells].add(
        jnp.broadcast_to(pump_value[:, None], pump_cells.shape)
    )
    source = flat_source.reshape(tests_here, size_x, size_y, size_z)
    heads_field = relax_field(source, conductance, diagonal)
    well_heads = jnp.mean(heads_field.reshape(tests_here, cell_count)[:, screen_cells], axis=2)
    residual = jnp.where(owned_here[None, :], well_heads - observed, 0.0)
    well_count = residual.shape[1]
    misfit = lax.psum(jnp.sum(residual * residual, axis=1), ("bx", "by")) / well_count + epsilon
    weights = residual / misfit[:, None]
    values = jnp.broadcast_to(weights[:, :, None], (tests_here, well_count, SCREEN)).reshape(
        tests_here, -1
    )
    adjoint_source = (
        jnp.zeros((tests_here, cell_count), jnp.float32).at[:, screen_cells.reshape(-1)].add(values)
    )
    adjoint_field = relax_field(
        adjoint_source.reshape(tests_here, size_x, size_y, size_z), conductance, diagonal
    )
    stacked = with_halo(
        jnp.concatenate([heads_field, adjoint_field], axis=0), (("bx", 1), ("by", 2)), 1
    )
    test_terms = sensitivity(
        conductance, heads_field, stacked[:tests_here], adjoint_field, stacked[tests_here:]
    )
    return (test_terms, misfit)


def local(
    log_conductivity,
    storage,
    recharge,
    pump_rate,
    pump_well,
    observed,
    owner,
    screen_column,
    screen_top,
):
    size_z = log_conductivity.shape[2]
    tests_here = pump_rate.shape[0]
    test_terms, misfit = per_sweep_terms(
        log_conductivity,
        storage,
        recharge,
        pump_rate,
        pump_well,
        observed,
        owner,
        screen_column,
        screen_top,
    )
    local_sum = jnp.sum(test_terms, axis=0)
    all_tests = tests_here * lax.axis_size("test")
    grand_total = lax.psum(local_sum, "test")
    slab_depth = size_z // lax.axis_size("test")
    gradient = lax.dynamic_slice_in_dim(
        grand_total, lax.axis_index("test") * slab_depth, slab_depth, 2
    )
    return gradient / all_tests


def solution(mesh):
    placed = (
        P("bx", "by", None),
        P("bx", "by", None),
        P("bx", "by", None),
        P("test"),
        P("test"),
        P("test", None),
        P(),
        P(),
        P(),
    )
    return jax.shard_map(
        local, mesh=mesh, in_specs=placed, out_specs=P("bx", "by", "test"), check_vma=False
    )
```

profile of v0, /device:TPU:1, one launch (start us, length us, event | category | flops | bytes accessed | tf_op | source)
XLA Modules:
  0.0 625.6 jit_solution(6473687219000279522)
XLA Ops:
  6.5 0.7 fusion.117
  7.3 4.0 collective-permute-start.1
  11.3 1.3 collective-permute-start
  12.6 0.7 compare_select_fusion.3
  13.3 0.7 multiply_add_fusion
  14.0 0.3 iota_add_fusion
  14.3 0.6 gather_fusion
  14.9 1.3 gather_fusion.1
  16.2 0.8 constant_dynamic-update-slice_fusion.1
  17.1 1.3 collective-permute-start.2
  18.4 4.0 collective-permute-start.3
  22.4 0.7 compare_select_fusion.4
  23.3 0.9 copy.25
  24.2 2.1 scatter_fusion
  26.4 1.2 add_add_fusion
  27.7 1.3 collective-permute-start.4
  29.0 4.6 collective-permute-start.5
  33.7 1.0 collective-permute-done.5
  34.7 1.3 collective-permute-start.6
  36.0 4.0 collective-permute-start.7
  40.0 0.3 compare_select_fusion
  40.4 0.5 reshape.131
  41.1 0.4 copy-done.11
  41.5 0.2 copy-done.12
  41.7 1.1 fusion.9
  42.8 1.3 collective-permute-start.8
  44.1 4.3 collective-permute-start.9
  48.4 1.0 collective-permute-done.9
  49.4 1.3 collective-permute-start.10
  50.7 4.3 collective-permute-start.11
  55.0 0.5 add.270
  55.6 1.1 copy.21
  56.7 0.3 fusion.15
  57.0 4.7 copy.20
  61.8 58.2 %gather_fusion.2 = f32[16384,4]{1,0:T(8,128)} fusion(f32[4,16384]{0,1:T(8,128)} %bitcast.34, s32[16384]{0:T(1024)S(1)} %broadcast_clamp_fusion), kind=kCustom, calls=%fused_computation.2 | custom fusion | bytes 589824 | tf_op jit(solution)/shard_map/gather | solution.py:101
  120.0 13.0 %bitcast_reduce_fusion = f32[2048,4]{1,0:T(8,128)S(1)} fusion(f32[16384,4]{1,0:T(8,128)} %gather_fusion.2), kind=kLoop, calls=%fused_computation.7 | loop fusion | flops 57344 | bytes 294912 | tf_op jit(solution)/shard_map/reduce_sum | solution.py:101
  133.0 0.5 multiply_reduce_fusion
  133.4 0.7 compare_select_fusion.1
  134.1 213.3 %psum.14 = f32[4]{0:T(128)S(1)} all-reduce(f32[4]{0:T(128)S(1)} %multiply_reduce_fusion), channel_id=1, replica_groups=mesh['test'=8,'bx'=4,'by'=16] {'bx','by'}, use_global_device_ids=true, to_apply=%region_3.4 | all-reduce | flops 4 | bytes 32 | tf_op jit(solution)/shard_map/psum | solution.py:104
  347.4 0.4 broadcast_divide_fusion
  347.9 91.6 %scatter_custom_fusion.1 = f32[4,16384]{0,1:T(8,128)} fusion(s32[16384]{0:T(1024)} %bitcast.41, f32[4,2048]{0,1:T(8,128)S(1)} %broadcast_divide_fusion, f32[]{:T(128)} %constant.27.clone.1), kind=kCustom, calls=%fused_computation.5 | custom fusion | flops 65536 | bytes 295424 | tf_op jit(solution)/shard_map/scatter-add | solution.py:110
  439.5 5.2 copy.24
  444.8 1.3 collective-permute-start.12
  446.1 4.0 collective-permute-start.13
  450.1 1.0 collective-permute-done.13
  451.1 1.3 collective-permute-start.14
  452.4 4.0 collective-permute-start.15
  456.4 1.1 collective-permute-done.15
  457.5 0.2 fusion.21
  457.8 1.3 collective-permute-start.16
  459.1 4.3 collective-permute-start.17
  463.4 1.0 collective-permute-done.17
  464.4 1.3 collective-permute-start.18
  465.7 4.3 collective-permute-start.19
  470.0 1.1 collective-permute-done.19
  471.4 1.3 collective-permute-start.20
  472.7 4.3 collective-permute-start.21
  476.9 1.3 collective-permute-done.21
  478.4 1.3 collective-permute-start.22
  479.6 4.3 collective-permute-start.23
  484.0 1.5 collective-permute-done.23
  485.4 1.1 fusion.35
  486.6 130.7 %all-reduce.9.cloned.1.call-done = f32[8,8,256]{2,1,0:T(8,128)} async-done(((f32[8,8,256]{2,1,0:T(8,128)}), f32[8,8,256]{2,1,0:T(8,128)}) %all-reduce.9.cloned.1.call-update) | async-done | bytes 65552 | tf_op jit(solution)/shard_map/psum | solution.py:150
  617.3 1.4 dynamic-slice_multiply_fusion
  (67 shorter events, 1.3 us)
Async XLA Ops:
  6.5 48.5 %copy-start = (s32[2048]{0:T(1024)S(1)}, s32[2048]{0:T(1024)}, u32[]{:S(2)}) copy-start(s32[2048]{0:T(1024)} %param.15) | copy-start | bytes 24580
  6.5 610.8 %all-reduce.9.cloned.1.call-start = ((), (), s32[]{:S(2)}) async-start(), calls=%async_computation | async-start | bytes 131072 | tf_op jit(solution)/shard_map/psum | solution.py:150
  7.3 9.0 %collective-permute-start.1 = (f32[1,8,256]{2,1,0:T(8,128)S(1)}, f32[1,8,256]{2,1,0:T(8,128)S(1)}, u32[]{:S(2)}, u32[]{:S(2)}) collective-permute-start(f32[1,8,256]{2,1,0:T(8,128)S(1)} %get-tuple-element.35), channel_id=1, source_target_pairs={{0,16},{16,32},{32,48},{1,17},{17,33},{33,49},{2,18},{18,34},{34,5... | collective-permute-start | bytes 24584 | tf_op jit(solution)/shard_map/ppermute | solution.py:18
  11.3 5.8 collective-permute-start
  17.1 9.3 %collective-permute-start.2 = (f32[10,1,256]{2,1,0:T(1,128)S(1)}, f32[10,1,256]{2,1,0:T(1,128)S(1)}, u32[]{:S(2)}, u32[]{:S(2)}) collective-permute-start(f32[10,1,256]{2,1,0:T(1,128)S(1)} %get-tuple-element.33), channel_id=1, source_target_pairs={{1,0},{2,1},{3,2},{4,3},{5,4},{6,5},{7,6},{8,7},{9,8},{10,9},{11,1... | collective-permute-start | bytes 30728 | tf_op jit(solution)/shard_map/ppermute | solution.py:21
  18.4 8.0 %collective-permute-start.3 = (f32[10,1,256]{2,1,0:T(1,128)S(1)}, f32[10,1,256]{2,1,0:T(1,128)S(1)}, u32[]{:S(2)}, u32[]{:S(2)}) collective-permute-start(f32[10,1,256]{2,1,0:T(1,128)S(1)} %get-tuple-element.32), channel_id=1, source_target_pairs={{0,1},{1,2},{2,3},{3,4},{4,5},{5,6},{6,7},{7,8},{8,9},{9,10},{10,1... | collective-permute-start | bytes 30728 | tf_op jit(solution)/shard_map/ppermute | solution.py:18
  27.6 34.1 %copy-start.1 = (f32[8,8,256]{2,1,0:T(8,128)}, f32[8,8,256]{2,1,0:T(8,128)S(1)}, u32[]{:S(2)}) copy-start(f32[8,8,256]{2,1,0:T(8,128)S(1)} %get-tuple-element.7) | copy-start | bytes 196612
  27.6 34.1 %copy-start.3 = (f32[8,8,256]{2,1,0:T(8,128)}, f32[8,8,256]{2,1,0:T(8,128)S(1)}, u32[]{:S(2)}) copy-start(f32[8,8,256]{2,1,0:T(8,128)S(1)} %get-tuple-element.8) | copy-start | bytes 196612
  27.6 34.1 %copy-start.5 = (f32[8,8,256]{2,1,0:T(8,128)}, f32[8,8,256]{2,1,0:T(8,128)S(1)}, u32[]{:S(2)}) copy-start(f32[8,8,256]{2,1,0:T(8,128)S(1)} %get-tuple-element.9) | copy-start | bytes 196612
  27.6 34.1 %copy-start.7 = (f32[8,8,256]{2,1,0:T(8,128)}, f32[8,8,256]{2,1,0:T(8,128)S(1)}, u32[]{:S(2)}) copy-start(f32[8,8,256]{2,1,0:T(8,128)S(1)} %get-tuple-element.10) | copy-start | bytes 196612
  27.7 34.1 %copy-start.9 = (f32[8,8,256]{2,1,0:T(8,128)}, f32[8,8,256]{2,1,0:T(8,128)S(1)}, u32[]{:S(2)}) copy-start(f32[8,8,256]{2,1,0:T(8,128)S(1)} %get-tuple-element.11) | copy-start | bytes 196612
  27.7 5.9 collective-permute-start.4
  29.0 5.6 collective-permute-start.5
  34.7 6.1 collective-permute-start.6
  36.0 5.1 collective-permute-start.7
  40.9 0.6 copy-start.11
  41.1 0.6 copy-start.12
  42.8 5.6 collective-permute-start.8
  44.1 5.3 collective-permute-start.9
  49.4 7.3 %collective-permute-start.10 = (f32[4,10,1,256]{3,2,1,0:T(1,128)S(1)}, f32[4,10,1,256]{3,2,1,0:T(1,128)S(1)}, u32[]{:S(2)}, u32[]{:S(2)}) collective-permute-start(f32[4,10,1,256]{3,2,1,0:T(1,128)S(1)} %get-tuple-element.20), channel_id=1, source_target_pairs={{1,0},{2,1},{3,2},{4,3},{5,4},{6,5},{7,6},{8,7},{9,8},{10,9},{11,1... | collective-permute-start | bytes 122888 | tf_op jit(solution)/shard_map/ppermute | solution.py:21
  50.7 6.0 collective-permute-start.11
  347.9 109.6 %copy-start.2 = (f32[8,8,256]{2,1,0:T(8,128)S(1)}, f32[8,8,256]{2,1,0:T(8,128)}, u32[]{:S(2)}) copy-start(f32[8,8,256]{2,1,0:T(8,128)} %copy-done.1) | copy-start | bytes 196612
  347.9 109.6 %copy-start.4 = (f32[8,8,256]{2,1,0:T(8,128)S(1)}, f32[8,8,256]{2,1,0:T(8,128)}, u32[]{:S(2)}) copy-start(f32[8,8,256]{2,1,0:T(8,128)} %copy-done.3) | copy-start | bytes 196612
  347.9 109.6 %copy-start.6 = (f32[8,8,256]{2,1,0:T(8,128)S(1)}, f32[8,8,256]{2,1,0:T(8,128)}, u32[]{:S(2)}) copy-start(f32[8,8,256]{2,1,0:T(8,128)} %copy-done.5) | copy-start | bytes 196612
  347.9 109.6 %copy-start.8 = (f32[8,8,256]{2,1,0:T(8,128)S(1)}, f32[8,8,256]{2,1,0:T(8,128)}, u32[]{:S(2)}) copy-start(f32[8,8,256]{2,1,0:T(8,128)} %copy-done.7) | copy-start | bytes 196612
  347.9 109.6 %copy-start.10 = (f32[8,8,256]{2,1,0:T(8,128)S(1)}, f32[8,8,256]{2,1,0:T(8,128)}, u32[]{:S(2)}) copy-start(f32[8,8,256]{2,1,0:T(8,128)} %copy-done.9) | copy-start | bytes 196612
  444.8 5.3 collective-permute-start.12
  446.1 5.0 collective-permute-start.13
  451.1 5.3 collective-permute-start.14
  452.4 5.1 collective-permute-start.15
  457.8 5.6 collective-permute-start.16
  459.1 5.3 collective-permute-start.17
  464.4 5.6 collective-permute-start.18
  465.7 5.4 collective-permute-start.19
  471.4 5.6 collective-permute-start.20
  472.7 5.6 collective-permute-start.21
  478.4 5.6 collective-permute-start.22
  479.6 5.8 collective-permute-start.23
Sparse Core Ops, SparseCore 0:
  486.7 130.5 all-reduce.8
where the time goes:
time: 628 us; the launch traced here: 626 us
  blocking collectives  213 us (34%)
  waiting for transfers between devices  140 us (22%)
  other arithmetic  117 us (19%)
  local copies, waits for them, and re-layouts  75.6 us (12%)
  starting transfers between devices  65.8 us (10%)
  between operations  14 us (2%)
    psum x1, blocking collectives, per_sweep_terms(): lax.psum(jnp.sum(residual * residual, axis=1), ('bx', 'by')) / well_count  213 us
    psum x1, waiting for transfers between devices, local(): grand_total = lax.psum(local_sum, 'test')  131 us
    scatter-add x1, other arithmetic, per_sweep_terms(): jnp.zeros((tests_here, cell_count), jnp.float32)  91.6 us
    gather x1, local copies, waits for them, and re-layouts, per_sweep_terms(): heads_field.reshape(tests_here, cell_count)[:, screen_cells]  58.2 us
    ppermute x12, starting transfers between devices, with_halo(): lax.ppermute(lax.slice_in_dim(block, block.shape[dim] - width, None, axis...  50.3 us
    ppermute x12, starting transfers between devices, with_halo(): lax.ppermute(lax.slice_in_dim(block, 0, width, axis=dim), axis, backward)  15.5 us
    reduce_sum x1, other arithmetic, per_sweep_terms(): jnp.mean(heads_field.reshape(tests_here, cell_count)[:, screen_cells], ax...  13 us
  transfers between devices with their start and end apart: 25, of which 10 were waited for; matrix products, arithmetic and copies ran while one was open for 2% of the time, Pallas kernels for 0%

commit v1 on v0

v1 whole, which is shorter than its diff:
```python
import functools

import jax
import jax.numpy as jnp
from jax import lax
from jax.experimental import pallas as pl
from jax.experimental.pallas import tpu as pltpu
from jax.sharding import PartitionSpec as P

F32 = jnp.float32
MESH = pl.DeviceIdType.MESH
VMEM = pltpu.VMEM
SMEM = pltpu.SMEM
HIGHEST = lax.Precision.HIGHEST
EPSILON = 1e-06
SCREEN = 8
SIDE = 8
HALO = 4
EXT = SIDE + 2 * HALO
NX_BRICKS, NY_BRICKS = 4, 16
ROUND = 4
TESTS_AXIS = 8
WELLS = 2048
OWN = 32
DIRECTIONS = [(dx, dy) for dx in (-1, 0, 1) for dy in (-1, 0, 1)]
NEIGHBOURS = [(k, d) for k, d in enumerate(DIRECTIONS) if d != (0, 0)]


def iota(shape, dim):
    return lax.broadcasted_iota(jnp.int32, shape, dim)


def z_neighbours(values, fill):
    sub, lane = iota(values.shape, 1), iota(values.shape, 2)
    low = pltpu.roll(values, 1, 2)
    low = jnp.where(lane == 0, jnp.where(sub < 4, fill, pltpu.roll(low, 4, 1)), low)
    high = pltpu.roll(values, 127, 2)
    high = jnp.where(lane == 127, jnp.where(sub < 4, pltpu.roll(high, 4, 1), fill), high)
    return low, high


def around(ref, x, lo, hi, fill):
    low, high = z_neighbours(ref[x, lo:hi], fill)
    return (
        (ref[x - 1, lo:hi] + ref[x + 1, lo:hi])
        + (ref[x, lo - 1 : hi - 1] + ref[x, lo + 1 : hi + 1])
        + (low + high)
    )


def rows(lo, hi, body):
    def step(x, carry):
        body(x)
        return carry

    lax.fori_loop(lo, hi, step, 0)


def halves(ref, x, lo, hi, field):
    first = ref[x, lo:hi, 2 * field : 2 * field + 1, :]
    second = ref[x, lo:hi, 2 * field + 1 : 2 * field + 2, :]
    shape = (hi - lo, 8, 128)
    return jnp.where(
        iota(shape, 1) < 4, jnp.broadcast_to(first, shape), jnp.broadcast_to(second, shape)
    )


def inside(x, lo, hi):
    shape = (hi - lo, 8, 128)
    gx = lax.axis_index("bx") * SIDE + x - HALO + jnp.zeros(shape, jnp.int32)
    gy = lax.axis_index("by") * SIDE + lo - HALO + iota(shape, 0)
    return (gx >= 0) & (gx < NX_BRICKS * SIDE) & (gy >= 0) & (gy < NY_BRICKS * SIDE)


def neighbour(dx, dy):
    bx, by = lax.axis_index("bx"), lax.axis_index("by")
    return {
        "bx": lax.rem(bx + dx + NX_BRICKS, NX_BRICKS),
        "by": lax.rem(by + dy + NY_BRICKS, NY_BRICKS),
    }


def span(step, width):
    if step == 0:
        return 0, HALO, SIDE
    if step > 0:
        return SIDE - width, HALO - width, width
    return 0, HALO + SIDE, width


def greet(peers):
    barrier = pltpu.get_barrier_semaphore()
    for peer in peers:
        pl.semaphore_signal(barrier, inc=1, device_id=peer, device_id_type=MESH)
    pl.semaphore_wait(barrier, len(peers))


def exchange_kernel(packed, ext, send_sems, recv_sems):
    for cx in (0, HALO + SIDE):
        for cy in (0, HALO + SIDE):
            ext[cx : cx + HALO, cy : cy + HALO] = jnp.zeros((HALO, HALO, 8, 128), F32)
    greet([neighbour(dx, dy) for k, (dx, dy) in NEIGHBOURS])
    copies = []
    for k, (dx, dy) in NEIGHBOURS:
        width = HALO if dx == 0 or dy == 0 else HALO - 1
        from_x, to_x, count_x = span(dx, width)
        from_y, to_y, count_y = span(dy, width)
        copies.append(
            pltpu.make_async_remote_copy(
                src_ref=packed.at[pl.ds(from_x, count_x), pl.ds(from_y, count_y)],
                dst_ref=ext.at[pl.ds(to_x, count_x), pl.ds(to_y, count_y)],
                send_sem=send_sems.at[k],
                recv_sem=recv_sems.at[k],
                device_id=neighbour(dx, dy),
                device_id_type=MESH,
            )
        )
        copies[-1].start()
    ext[HALO : HALO + SIDE, HALO : HALO + SIDE] = packed[...]
    for copy in copies:
        copy.wait()


def coefficients(ext, e_ref, r_ref, alpha_ref, beta_ref, pump_cell, pump_tile):
    def roots(x):
        e_ref[x] = jnp.where(inside(x, 0, EXT), jnp.exp(0.5 * halves(ext, x, 0, EXT, 0)), 1.0)

    rows(0, EXT, roots)
    lo, hi = 1, EXT - 1

    def terms(x):
        e = e_ref[x, lo:hi]
        diagonal = halves(ext, x, lo, hi, 1) + e * around(e_ref, x, lo, hi, 1.0)
        r = jnp.where(inside(x, lo, hi), 1.0 / diagonal, 0.0)
        cell = x * EXT + lo + iota(e.shape, 0)
        source = halves(ext, x, lo, hi, 2) + jnp.where(pump_cell[None] == cell, pump_tile[None], 0.0)
        er = e * r
        r_ref[x, lo:hi] = r
        alpha_ref[x, lo:hi] = e * er
        beta_ref[x, lo:hi] = er * source

    rows(lo, hi, terms)


def sweeps(e_ref, alpha_ref, beta_ref, u_ref, out_ref):
    def second(x):
        u_ref[x, 2 : EXT - 2] = beta_ref[x, 2 : EXT - 2] + alpha_ref[x, 2 : EXT - 2] * around(
            beta_ref, x, 2, EXT - 2, 0.0
        )

    rows(2, EXT - 2, second)

    def third(x):
        u = beta_ref[x, 3 : EXT - 3] + alpha_ref[x, 3 : EXT - 3] * around(u_ref, x, 3, EXT - 3, 0.0)
        out_ref[x, 3 : EXT - 3] = u / e_ref[x, 3 : EXT - 3]

    rows(3, EXT - 3, third)


def pumping(pump_rate, pump_well, owner, column, top):
    sub, lane = iota((8, 128), 0), iota((8, 128), 1)
    z = lane + jnp.where(sub < 4, 0, 128)
    cell = jnp.zeros((8, 128), jnp.int32)
    tile = jnp.zeros((8, 128), F32)
    first_x = lax.axis_index("bx") * SIDE - HALO
    first_y = lax.axis_index("by") * SIDE - HALO
    for t in range(4):
        well = pump_well[t]
        brick, place, start = owner[well], column[well], top[well]
        x = (brick >> 4) * SIDE + (place >> 3) - first_x
        y = (brick & 15) * SIDE + (place & 7) - first_y
        ok = (x >= 0) & (x < EXT) & (y >= 0) & (y < EXT)
        mine = (sub & 3) == t
        cell = jnp.where(mine, jnp.where(ok, x * EXT + y, -1), cell)
        hit = mine & (z >= start) & (z < start + SCREEN)
        tile = jnp.where(hit, -pump_rate[t], tile)
    return cell, tile


def own_wells(owner, column, top, observed):
    brick = lax.axis_index("bx") * NY_BRICKS + lax.axis_index("by")
    mine = jnp.where(owner[...] == brick, 1.0, 0.0)
    upto = jnp.where(iota((128, 128), 0) <= iota((128, 128), 1), 1.0, 0.0)
    inner = jnp.dot(mine, upto, precision=HIGHEST, preferred_element_type=F32)
    count = jnp.broadcast_to(jnp.sum(mine, axis=1, keepdims=True), (16, 128))
    before = jnp.where(iota((16, 16), 1) < iota((16, 16), 0), 1.0, 0.0)
    rank = inner + jnp.dot(before, count, precision=HIGHEST, preferred_element_type=F32) - 1.0
    rank = jnp.where(mine > 0.0, rank, -1.0)
    place = iota((OWN, 128), 0).astype(F32)
    sums = [jnp.zeros((OWN, 128), F32) for field in range(6)]
    for k in range(16):
        hit = jnp.broadcast_to(rank[k : k + 1, :], (OWN, 128)) == place
        values = [column[k : k + 1, :].astype(F32), top[k : k + 1, :].astype(F32)]
        values += [observed[t : t + 1, k * 128 : (k + 1) * 128] for t in range(4)]
        for field in range(6):
            sums[field] = sums[field] + jnp.where(
                hit, jnp.broadcast_to(values[field], (OWN, 128)), 0.0
            )
    return [jnp.sum(s, axis=1, keepdims=True) for s in sums]


def residuals(heads_ref, wells, message, squares):
    column, top, observed = wells[0], wells[1], wells[2:]
    column2 = jnp.concatenate([column, column], axis=0)
    top2 = jnp.concatenate([top, top], axis=0)
    half = iota((2 * OWN, 128), 0) // OWN
    z = (iota((2 * OWN, 128), 1) + 128 * half).astype(F32)
    screen = jnp.where((z >= top2) & (z < top2 + SCREEN), 1.0, 0.0)
    heads = heads_ref[HALO : HALO + SIDE, HALO : HALO + SIDE].reshape(512, 128)
    sums = lax.dot_general(
        screen, heads, (((1,), (1,)), ((), ())), precision=HIGHEST, preferred_element_type=F32
    )
    at = iota((2 * OWN, 512), 1)
    keep = ((at >> 3).astype(F32) == column2) & (
        ((at >> 2) & 1) == iota((2 * OWN, 512), 0) // OWN
    )
    sums = jnp.where(keep, sums, 0.0)
    pick = jnp.where((iota((512, 128), 0) & 3) == iota((512, 128), 1), 1.0, 0.0)
    sums = jnp.dot(sums, pick, precision=HIGHEST, preferred_element_type=F32)
    sums = (sums[:OWN] + sums[OWN:]) * (1.0 / SCREEN)
    lane = iota((OWN, 128), 1)
    for t in range(4):
        sums = jnp.where(lane == t, sums - observed[t], sums)
    sums = jnp.where(lane == 4, column, sums)
    sums = jnp.where(lane == 5, top, sums)
    eye = jnp.where(iota((8, 128), 0) == iota((8, 128), 1), 1.0, 0.0)
    turned = lax.dot_general(
        eye, sums, (((1,), (1,)), ((), ())), precision=HIGHEST, preferred_element_type=F32
    )
    message[...] = jnp.concatenate([turned, jnp.zeros((8, 128 - OWN), F32)], axis=1)
    total = jnp.broadcast_to(jnp.sum(turned * turned, axis=1, keepdims=True), (8, 128))
    squares[...] = jnp.where(iota((8, 128), 0) < 4, total, pltpu.roll(total, 4, 0))


def heads_kernel(
    ext, owner, column, top, observed, owner_s, column_s, top_s, pump_rate, pump_well,
    e_ref, r_ref, alpha_ref, heads_ref, message, squares, beta_ref, u_ref,
):
    pump_cell, pump_tile = pumping(pump_rate, pump_well, owner_s, column_s, top_s)
    coefficients(ext, e_ref, r_ref, alpha_ref, beta_ref, pump_cell, pump_tile)
    sweeps(e_ref, alpha_ref, beta_ref, u_ref, heads_ref)
    residuals(heads_ref, own_wells(owner, column, top, observed), message, squares)


def residual_exchange_kernel(
    message, squares, messages, total, near, partial, far, msg_send, msg_recv, near_send, near_recv,
    far_send, far_recv,
):
    bx, by = lax.axis_index("bx"), lax.axis_index("by")
    turn, place = by // ROUND, lax.rem(by, ROUND)
    near_peers = [
        {
            "bx": lax.rem(bx + a, NX_BRICKS),
            "by": turn * ROUND + lax.rem(place + b, ROUND),
        }
        for a in range(NX_BRICKS) for b in range(ROUND) if a + b > 0
    ]
    far_count = NY_BRICKS // ROUND
    far_peers = [{"by": lax.rem(by + c * ROUND, NY_BRICKS)} for c in range(1, far_count)]
    greet([neighbour(dx, dy) for k, (dx, dy) in NEIGHBOURS] + near_peers + far_peers)
    copies = []

    def send(source, target, send_sem, recv_sem, peer):
        copy = pltpu.make_async_remote_copy(
            src_ref=source, dst_ref=target, send_sem=send_sem, recv_sem=recv_sem,
            device_id=peer, device_id_type=MESH,
        )
        copy.start()
        return copy

    near_copies = [
        send(squares, near.at[i], near_send.at[i], near_recv.at[i], peer)
        for i, peer in enumerate(near_peers)
    ]
    copies = [
        send(message, messages.at[8 - k], msg_send.at[k], msg_recv.at[k], neighbour(dx, dy))
        for k, (dx, dy) in NEIGHBOURS
    ]
    messages[4] = message[...]
    for copy in near_copies:
        copy.wait()
    here = squares[...]
    for i in range(len(near_peers)):
        here = here + near[i]
    partial[...] = here
    far_copies = [
        send(partial, far.at[i], far_send.at[i], far_recv.at[i], peer)
        for i, peer in enumerate(far_peers)
    ]
    for copy in far_copies + copies:
        copy.wait()
    for i in range(len(far_peers)):
        here = here + far[i]
    total[...] = here


def adjoint_source(messages, e_ref, r_ref, beta_ref, lhs):
    sub, lane = iota((8, 128), 0), iota((8, 128), 1)
    values = [jnp.zeros((8, 128), F32) for g in range(3)]
    cells = [jnp.zeros((8, 128), F32) for g in range(3)]
    tops = [jnp.zeros((8, 128), F32) for g in range(3)]
    for k, (dx, dy) in enumerate(DIRECTIONS):
        tile = messages[k]
        value = jnp.where(sub < 4, tile, pltpu.roll(tile, 4, 0))
        column = jnp.broadcast_to(tile[4:5], (8, 128))
        along = jnp.floor(column * (1.0 / SIDE))
        x = along + (HALO + SIDE * dx)
        y = column - along * SIDE + (HALO + SIDE * dy)
        ok = (x >= 1) & (x < EXT - 1) & (y >= 1) & (y < EXT - 1) & (lane < OWN)
        cell = jnp.where(ok, x * EXT + y, 0.0)
        top = jnp.where(lane < OWN, jnp.broadcast_to(tile[5:6], (8, 128)), 0.0)
        g, shift = k // 4, OWN * (k % 4)
        if shift:
            value, cell, top = [pltpu.roll(v, shift, 1) for v in (value, cell, top)]
        values[g], cells[g], tops[g] = values[g] + value, cells[g] + cell, tops[g] + top
    z = iota((256, 128), 0).astype(F32)
    screens = []
    for g in range(3):
        top = jnp.broadcast_to(tops[g][0:1], (256, 128))
        screens.append(jnp.where((z >= top) & (z < top + SCREEN), 1.0, 0.0))
    screen = jnp.concatenate(screens, axis=1)
    wide = EXT - 2
    shape = (wide, 8, 128)
    lo, hi = 1, EXT - 1

    def left(x):
        cell = (x * EXT + 1 + iota(shape, 0)).astype(F32)
        for g in range(3):
            lhs[x - 1, :, g * 128 : (g + 1) * 128] = jnp.where(
                cells[g][None] == cell, values[g][None], 0.0
            ).reshape(wide * 8, 128)

    rows(lo, hi, left)
    group = 7
    for first in range(0, wide, group):
        block = lhs[first : first + group].reshape(group * wide * 8, 384)
        both = lax.dot_general(
            block, screen, (((1,), (1,)), ((), ())), precision=HIGHEST, preferred_element_type=F32
        )
        pair = both.reshape(group, wide, 8, 256)
        for i in range(group):
            source = jnp.where(iota(shape, 1) < 4, pair[i, :, :, :128], pair[i, :, :, 128:])
            x = first + i + 1
            beta_ref[x, lo:hi] = e_ref[x, lo:hi] * r_ref[x, lo:hi] * source


def sensitivity(e_ref, heads_ref, adjoint_ref, scale, out_ref):
    lo, hi = HALO, HALO + SIDE

    def cell_terms(x):
        h, a = heads_ref[x, lo:hi], adjoint_ref[x, lo:hi]
        e = e_ref[x, lo:hi]
        total = jnp.zeros_like(h)
        for step_x, step_y in ((1, 0), (-1, 0), (0, 1), (0, -1)):
            at = (x + step_x, slice(lo + step_y, hi + step_y))
            total = total + e_ref[at] * (h - heads_ref[at]) * (a - adjoint_ref[at])
        for e_n, h_n, a_n in zip(
            z_neighbours(e, 1.0), z_neighbours(h, 0.0), z_neighbours(a, 0.0)
        ):
            total = total + e_n * (h - h_n) * (a - a_n)
        total = total * e * scale[None]
        total = total + pltpu.roll(total, 7, 1)
        out_ref[x - HALO] = total + pltpu.roll(total, 6, 1)

    rows(lo, hi, cell_terms)


def slabs(sum_ref, out):
    lane = iota((8, 128), 1)
    for half in range(2):
        planes = sum_ref[:, :, 4 * half, :]
        for q in range(4):
            for xq in range(2):
                packed = jnp.zeros((8, 128), F32)
                for xx in range(4):
                    plane = planes[4 * xq + xx]
                    shift = (32 * (xx - q)) % 128
                    if shift:
                        plane = pltpu.roll(plane, shift, 1)
                    packed = jnp.where((lane >> 5) == xx, plane, packed)
                out[4 * half + q, xq] = packed


def adjoint_kernel(
    e_ref, r_ref, alpha_ref, heads_ref, messages, total, out, beta_ref, u_ref, adjoint_ref, sum_ref, lhs
):
    adjoint_source(messages, e_ref, r_ref, beta_ref, lhs)
    sweeps(e_ref, alpha_ref, beta_ref, u_ref, adjoint_ref)
    scale = (-0.5 / (4 * TESTS_AXIS)) / (total[...] / WELLS + EPSILON)
    sensitivity(e_ref, heads_ref, adjoint_ref, scale, sum_ref)
    slabs(sum_ref, out)


def reduce_kernel(parts, out, slots, send_sems, recv_sems):
    me = lax.axis_index("test")
    peers = [lax.rem(me + d, TESTS_AXIS) for d in range(1, TESTS_AXIS)]
    greet([{"test": peer} for peer in peers])
    copies = []
    for i, peer in enumerate(peers):
        copies.append(
            pltpu.make_async_remote_copy(
                src_ref=parts.at[peer],
                dst_ref=slots.at[i],
                send_sem=send_sems.at[i],
                recv_sem=recv_sems.at[i],
                device_id={"test": peer},
                device_id_type=MESH,
            )
        )
        copies[-1].start()
    for copy in copies:
        copy.wait()
    total = parts[me]
    for i in range(TESTS_AXIS - 1):
        total = total + slots[i]
    for xq in range(2):
        for xx in range(4):
            plane = total[xq]
            if xx:
                plane = pltpu.roll(plane, 128 - 32 * xx, 1)
            out[4 * xq + xx] = plane[:, :32]


def call(kernel, inputs, outputs, scratch, *args, collective_id=None):
    remote = {} if collective_id is None else dict(collective_id=collective_id, has_side_effects=True)
    specs = [pl.BlockSpec(memory_space=space) for space in inputs]
    shapes = [jax.ShapeDtypeStruct(shape, F32) for shape in outputs]
    out_specs = [pl.BlockSpec(memory_space=VMEM) for shape in outputs]
    return pl.pallas_call(
        kernel,
        out_shape=shapes,
        in_specs=specs,
        out_specs=out_specs,
        scratch_shapes=scratch,
        compiler_params=pltpu.CompilerParams(vmem_limit_bytes=48 * 1024 * 1024, **remote),
    )(*args)


def local(
    log_conductivity, storage, recharge, pump_rate, pump_well, observed, owner, screen_column, screen_top
):
    dma = pltpu.SemaphoreType.DMA
    field = (EXT, EXT, 8, 128)
    tile = (8, 128)
    shape = (SIDE, SIDE, 2, 128)
    packed = jnp.concatenate(
        [log_conductivity.reshape(shape), storage.reshape(shape), recharge.reshape(shape),
         jnp.zeros(shape, F32)],
        axis=2,
    )
    (ext,) = call(
        exchange_kernel, [VMEM], [field], [dma((9,)), dma((9,))], packed, collective_id=0
    )
    table = [a.reshape(16, 128) for a in (owner, screen_column, screen_top)]
    e, r, alpha, heads, message, squares = call(
        heads_kernel, [VMEM] * 5 + [SMEM] * 5, [field] * 4 + [tile] * 2,
        [VMEM(field, F32), VMEM(field, F32)],
        ext, *table, observed, owner, screen_column, screen_top, pump_rate, pump_well,
    )
    near, far = NX_BRICKS * ROUND - 1, NY_BRICKS // ROUND - 1
    messages, total = call(
        residual_exchange_kernel, [VMEM] * 2, [(9,) + tile, tile],
        [VMEM((near,) + tile, F32), VMEM(tile, F32), VMEM((far,) + tile, F32),
         dma((9,)), dma((9,)), dma((near,)), dma((near,)), dma((far,)), dma((far,))],
        message, squares, collective_id=1,
    )
    (parts,) = call(
        adjoint_kernel, [VMEM] * 6, [(TESTS_AXIS, 2) + tile],
        [VMEM(field, F32), VMEM(field, F32), VMEM(field, F32), VMEM((SIDE, SIDE) + tile, F32),
         VMEM((EXT - 2, (EXT - 2) * 8, 384), F32)],
        e, r, alpha, heads, messages, total,
    )
    (gradient,) = call(
        reduce_kernel, [VMEM], [(SIDE, SIDE, 32)],
        [VMEM((TESTS_AXIS - 1, 2) + tile, F32), dma((TESTS_AXIS - 1,)), dma((TESTS_AXIS - 1,))],
        parts, collective_id=2,
    )
    return gradient


def solution(mesh):
    placed = (
        P("bx", "by", None), P("bx", "by", None), P("bx", "by", None), P("test"), P("test"),
        P("test", None), P(), P(), P(),
    )
    return jax.shard_map(
        local, mesh=mesh, in_specs=placed, out_specs=P("bx", "by", "test"), check_vma=False
    )
```

time: 628 us -> 79.3 us (0.13)
  blocking collectives: 213 us -> 0 us
  waiting for transfers between devices: 140 us -> 0 us
  other arithmetic: 117 us -> 0.1 us
  Pallas kernels: 0 us -> 76.2 us
  local copies, waits for them, and re-layouts: 75.6 us -> 2.5 us
  starting transfers between devices: 65.8 us -> 0 us
  between operations: 14 us -> 0.17 us
    psum x1 -> x0, blocking collectives: 213 us -> none  [per_sweep_terms(): lax.psum(jnp.sum(residual * residual, axis=1), ('bx', 'by')) / well_count]
    psum x1 -> x0, waiting for transfers between devices: 131 us -> none  [local(): grand_total = lax.psum(local_sum, 'test')]
    scatter-add x2 -> x0, other arithmetic: 93.7 us -> none  [the longest x1 91.6 us: per_sweep_terms(): jnp.zeros((tests_here, cell_count), jnp.float32)]
    pallas_call x0 -> x5, Pallas kernels: none -> 76.2 us  [call(): pl.pallas_call(kernel, out_shape=shapes, in_specs=specs, out_specs=out_sp...]
    ppermute x24 -> x0, starting transfers between devices: 65.8 us -> none  [the longest x12 50.3 us: with_halo(): lax.ppermute(lax.slice_in_dim(block, block.shape[dim] - width, None, axis...]
    gather x3 -> x0, local copies, waits for them, and re-layouts: 60.1 us -> none  [the longest x1 58.2 us: per_sweep_terms(): heads_field.reshape(tests_here, cell_count)[:, screen_cells]]
    reduce_sum x3 -> x0, other arithmetic: 14.6 us -> none  [the longest x1 13 us: per_sweep_terms(): jnp.mean(heads_field.reshape(tests_here, cell_count)[:, screen_cells], ax...]
    ppermute x24 -> x0, waiting for transfers between devices: 9.11 us -> none  [the longest x12 9.08 us: with_halo(): lax.ppermute(lax.slice_in_dim(block, block.shape[dim] - width, None, axis...]
  transfers between devices with their start and end apart: 25 -> 0, of which waited for: 10 -> 0; matrix products, arithmetic and copies ran while one was open for 2% -> 0% of each run, Pallas kernels for 0% -> 0%
where the time goes in v1:
time: 79.3 us; the launch traced here: 79 us
  Pallas kernels  76.2 us (96%)
  local copies, waits for them, and re-layouts  2.5 us (3%)
    pallas_call x5, Pallas kernels, call(): pl.pallas_call(kernel, out_shape=shapes, in_specs=specs, out_specs=out_sp...  76.2 us

profile of v1, /device:TPU:1, one launch (start us, length us, event | category | flops | bytes accessed | tf_op | source)
XLA Modules:
  0.0 79.0 jit_solution(9683158245252190709)
XLA Ops:
  0.0 0.1 pad.3.clone
  0.1 0.0 copy-start.6
  0.1 0.9 %reshape.18 = f32[8,8,2,128]{3,2,1,0:T(2,128)S(1)} reshape(f32[8,8,256]{2,1,0:T(8,128)} %param.9) | data formatting | bytes 131072 | tf_op jit(solution)/shard_map/reshape | solution.py:447
  1.0 0.0 copy-done.6
  1.0 0.0 copy-start.7
  1.1 0.8 copy-done.7
  1.9 0.1 maximum_maximum_fusion.packed
  2.0 0.0 copy-start
  2.0 0.0 copy-start.1
  2.0 0.0 copy-start.2
  2.0 0.0 copy-start.3
  2.0 0.0 copy-start.4
  2.0 0.0 copy-start.5
  2.1 34.6 %shard_map.91.ext = f32[16,16,8,128]{3,2,1,0:T(8,128)S(1)} custom-call(f32[8,8,8,128]{3,2,1,0:T(8,128)S(1)} %maximum_maximum_fusion.packed), custom_call_target="tpu_custom_call" | custom-call | tf_op jit(solution)/shard_map/pallas_call | solution.py:429
  36.7 0.0 copy-done
  36.7 0.0 copy-done.1
  36.7 0.0 copy-done.2
  36.7 0.0 copy-done.3
  36.7 0.0 copy-done.4
  36.7 0.0 copy-done.5
  36.7 6.8 %shard_map.92 = (f32[16,16,8,128]{3,2,1,0:T(8,128)S(1)}, f32[16,16,8,128]{3,2,1,0:T(8,128)S(1)}, f32[16,16,8,128]{3,2,1,0:T(8,128)S(1)}, f32[16,16,8,128]{3,2,1,...) custom-call(f32[16,16,8,128]{3,2,1,0:T(8,128)S(1)} %shard_map.91.ext, s32[16,128]{1,0:T(8,128)S(1)} %bitcast.3, ...), custom_call_target="tpu_custom_call" | custom-call | tf_op jit(solution)/shard_map/pallas_call | solution.py:429
  43.5 18.1 %shard_map.93 = (f32[9,8,128]{2,1,0:T(8,128)S(1)}, f32[8,128]{1,0:T(8,128)S(1)}) custom-call(f32[8,128]{1,0:T(8,128)S(1)} %get-tuple-element.17.message, f32[8,128]{1,0:T(8,128)S(1)} %get-tuple-element.18.squares), custom_call_target="tpu_custom_call" | custom-call | tf_op jit(solution)/shard_map/pallas_call | solution.py:429
  61.7 6.5 %shard_map.94.parts = f32[8,2,8,128]{3,2,1,0:T(8,128)S(1)} custom-call(f32[16,16,8,128]{3,2,1,0:T(8,128)S(1)} %get-tuple-element.13.e_ref, f32[16,16,8,128]{3,2,1,0:T(8,128)S(1)} %get-tuple-element.14.r_ref, f32[16,16,8,128]{3,2,1,0:T(8,128)S(1)} %get-tuple-element.15.alpha_ref, f32[16,16,8,128]{3,2,1,0:T(8,128)S(1)} %get-tuple-element.16.heads_ref, ...), custom_call_target="tpu_custom_call" | custom-call | tf_op jit(solution)/shard_map/pallas_call | solution.py:429
  68.2 10.2 %shard_map.95 = f32[8,8,32]{2,1,0:T(8,128)S(1)} custom-call(f32[8,2,8,128]{3,2,1,0:T(8,128)S(1)} %shard_map.94.parts), custom_call_target="tpu_custom_call" | custom-call | tf_op jit(solution)/shard_map/pallas_call | solution.py:429
  78.4 0.6 copy.11
  (3 shorter events, 0.1 us)
Async XLA Ops:
  0.1 0.9 %copy-start.6 = (f32[8,8,256]{2,1,0:T(8,128)S(1)}, f32[8,8,256]{2,1,0:T(8,128)}, u32[]{:S(2)}) copy-start(f32[8,8,256]{2,1,0:T(8,128)} %param.10) | copy-start | bytes 196612
  1.0 0.8 %copy-start.7 = (f32[8,8,256]{2,1,0:T(8,128)S(1)}, f32[8,8,256]{2,1,0:T(8,128)}, u32[]{:S(2)}) copy-start(f32[8,8,256]{2,1,0:T(8,128)} %param.11) | copy-start | bytes 196612
  2.0 34.7 %copy-start = (s32[2048]{0:T(1024)S(1)}, s32[2048]{0:T(1024)}, u32[]{:S(2)}) copy-start(s32[2048]{0:T(1024)} %owner_s.1) | copy-start | bytes 24580
  2.0 34.7 %copy-start.1 = (s32[2048]{0:T(1024)S(1)}, s32[2048]{0:T(1024)}, u32[]{:S(2)}) copy-start(s32[2048]{0:T(1024)} %column_s.1) | copy-start | bytes 24580
  2.0 34.7 %copy-start.2 = (s32[2048]{0:T(1024)S(1)}, s32[2048]{0:T(1024)}, u32[]{:S(2)}) copy-start(s32[2048]{0:T(1024)} %top_s.1) | copy-start | bytes 24580
  2.0 34.7 %copy-start.3 = (f32[4,2048]{1,0:T(4,128)S(1)}, f32[4,2048]{1,0:T(4,128)}, u32[]{:S(2)}) copy-start(f32[4,2048]{1,0:T(4,128)} %observed.1) | copy-start | bytes 98308
  2.0 34.7 %copy-start.4 = (f32[4]{0:T(128)S(1)}, f32[4]{0:T(128)}, u32[]{:S(2)}) copy-start(f32[4]{0:T(128)} %pump_rate.1) | copy-start | bytes 52
  2.0 34.7 %copy-start.5 = (s32[4]{0:T(128)S(1)}, s32[4]{0:T(128)}, u32[]{:S(2)}) copy-start(s32[4]{0:T(128)} %pump_well.1) | copy-start | bytes 52

commit v2 on v1

--- a/solution.py
+++ b/solution.py
@@ -1,5 +1,3 @@
-import functools
-
 import jax
 import jax.numpy as jnp
 from jax import lax
@@ -88,37 +86,29 @@
     return 0, HALO + SIDE, width
 
 
-def greet(peers):
-    barrier = pltpu.get_barrier_semaphore()
-    for peer in peers:
-        pl.semaphore_signal(barrier, inc=1, device_id=peer, device_id_type=MESH)
-    pl.semaphore_wait(barrier, len(peers))
-
-
-def exchange_kernel(packed, ext, send_sems, recv_sems):
-    for cx in (0, HALO + SIDE):
-        for cy in (0, HALO + SIDE):
-            ext[cx : cx + HALO, cy : cy + HALO] = jnp.zeros((HALO, HALO, 8, 128), F32)
-    greet([neighbour(dx, dy) for k, (dx, dy) in NEIGHBOURS])
+def remote(source, target, send_sem, recv_sem, peer):
+    copy = pltpu.make_async_remote_copy(
+        src_ref=source, dst_ref=target, send_sem=send_sem, recv_sem=recv_sem,
+        device_id=peer, device_id_type=MESH,
+    )
+    copy.start()
+    return copy
+
+
+def start_halos(packed, ext, send_sems, recv_sems):
     copies = []
     for k, (dx, dy) in NEIGHBOURS:
         width = HALO if dx == 0 or dy == 0 else HALO - 1
         from_x, to_x, count_x = span(dx, width)
         from_y, to_y, count_y = span(dy, width)
         copies.append(
-            pltpu.make_async_remote_copy(
-                src_ref=packed.at[pl.ds(from_x, count_x), pl.ds(from_y, count_y)],
-                dst_ref=ext.at[pl.ds(to_x, count_x), pl.ds(to_y, count_y)],
-                send_sem=send_sems.at[k],
-                recv_sem=recv_sems.at[k],
-                device_id=neighbour(dx, dy),
-                device_id_type=MESH,
+            remote(
+                packed.at[pl.ds(from_x, count_x), pl.ds(from_y, count_y)],
+                ext.at[pl.ds(to_x, count_x), pl.ds(to_y, count_y)],
+                send_sems.at[k], recv_sems.at[k], neighbour(dx, dy),
             )
         )
-        copies[-1].start()
-    ext[HALO : HALO + SIDE, HALO : HALO + SIDE] = packed[...]
-    for copy in copies:
-        copy.wait()
+    return copies
 
 
 def coefficients(ext, e_ref, r_ref, alpha_ref, beta_ref, pump_cell, pump_tile):
@@ -230,68 +220,6 @@
     message[...] = jnp.concatenate([turned, jnp.zeros((8, 128 - OWN), F32)], axis=1)
     total = jnp.broadcast_to(jnp.sum(turned * turned, axis=1, keepdims=True), (8, 128))
     squares[...] = jnp.where(iota((8, 128), 0) < 4, total, pltpu.roll(total, 4, 0))
-
-
-def heads_kernel(
-    ext, owner, column, top, observed, owner_s, column_s, top_s, pump_rate, pump_well,
-    e_ref, r_ref, alpha_ref, heads_ref, message, squares, beta_ref, u_ref,
-):
-    pump_cell, pump_tile = pumping(pump_rate, pump_well, owner_s, column_s, top_s)
-    coefficients(ext, e_ref, r_ref, alpha_ref, beta_ref, pump_cell, pump_tile)
-    sweeps(e_ref, alpha_ref, beta_ref, u_ref, heads_ref)
-    residuals(heads_ref, own_wells(owner, column, top, observed), message, squares)
-
-
-def residual_exchange_kernel(
-    message, squares, messages, total, near, partial, far, msg_send, msg_recv, near_send, near_recv,
-    far_send, far_recv,
-):
-    bx, by = lax.axis_index("bx"), lax.axis_index("by")
-    turn, place = by // ROUND, lax.rem(by, ROUND)
-    near_peers = [
-        {
-            "bx": lax.rem(bx + a, NX_BRICKS),
-            "by": turn * ROUND + lax.rem(place + b, ROUND),
-        }
-        for a in range(NX_BRICKS) for b in range(ROUND) if a + b > 0
-    ]
-    far_count = NY_BRICKS // ROUND
-    far_peers = [{"by": lax.rem(by + c * ROUND, NY_BRICKS)} for c in range(1, far_count)]
-    greet([neighbour(dx, dy) for k, (dx, dy) in NEIGHBOURS] + near_peers + far_peers)
-    copies = []
-
-    def send(source, target, send_sem, recv_sem, peer):
-        copy = pltpu.make_async_remote_copy(
-            src_ref=source, dst_ref=target, send_sem=send_sem, recv_sem=recv_sem,
-            device_id=peer, device_id_type=MESH,
-        )
-        copy.start()
-        return copy
-
-    near_copies = [
-        send(squares, near.at[i], near_send.at[i], near_recv.at[i], peer)
-        for i, peer in enumerate(near_peers)
-    ]
-    copies = [
-        send(message, messages.at[8 - k], msg_send.at[k], msg_recv.at[k], neighbour(dx, dy))
-        for k, (dx, dy) in NEIGHBOURS
-    ]
-    messages[4] = message[...]
-    for copy in near_copies:
-        copy.wait()
-    here = squares[...]
-    for i in range(len(near_peers)):
-        here = here + near[i]
-    partial[...] = here
-    far_copies = [
-        send(partial, far.at[i], far_send.at[i], far_recv.at[i], peer)
-        for i, peer in enumerate(far_peers)
-    ]
-    for copy in far_copies + copies:
-        copy.wait()
-    for i in range(len(far_peers)):
-        here = here + far[i]
-    total[...] = here
 
 
 def adjoint_source(messages, e_ref, r_ref, beta_ref, lhs):
@@ -381,34 +309,80 @@
                 out[4 * half + q, xq] = packed
 
 
-def adjoint_kernel(
-    e_ref, r_ref, alpha_ref, heads_ref, messages, total, out, beta_ref, u_ref, adjoint_ref, sum_ref, lhs
+def kernel(
+    packed, owner, column, top, observed, owner_s, column_s, top_s, pump_rate, pump_well, out,
+    ext, e_ref, r_ref, alpha_ref, heads_ref, beta_ref, u_ref, adjoint_ref, sum_ref, lhs,
+    message, squares, messages, near, partial, far, parts, slots,
+    halo_send, halo_recv, msg_send, msg_recv, near_send, near_recv, far_send, far_recv,
+    part_send, part_recv,
 ):
+    me, bx, by = lax.axis_index("test"), lax.axis_index("bx"), lax.axis_index("by")
+    turn, place = by // ROUND, lax.rem(by, ROUND)
+    neighbours = [neighbour(dx, dy) for k, (dx, dy) in NEIGHBOURS]
+    near_peers = [
+        {
+            "bx": lax.rem(bx + a, NX_BRICKS),
+            "by": turn * ROUND + lax.rem(place + b, ROUND),
+        }
+        for a in range(NX_BRICKS) for b in range(ROUND) if a + b > 0
+    ]
+    far_peers = [
+        {"by": lax.rem(by + c * ROUND, NY_BRICKS)} for c in range(1, NY_BRICKS // ROUND)
+    ]
+    test_peers = [lax.rem(me + d, TESTS_AXIS) for d in range(1, TESTS_AXIS)]
+    for cx in (0, HALO + SIDE):
+        for cy in (0, HALO + SIDE):
+            ext[cx : cx + HALO, cy : cy + HALO] = jnp.zeros((HALO, HALO, 8, 128), F32)
+    everyone = far_peers + neighbours + near_peers + [{"test": peer} for peer in test_peers]
+    barrier = pltpu.get_barrier_semaphore()
+    for peer in everyone:
+        pl.semaphore_signal(barrier, inc=1, device_id=peer, device_id_type=MESH)
+    pl.semaphore_wait(barrier, len(everyone))
+    halo_copies = start_halos(packed, ext, halo_send, halo_recv)
+    ext[HALO : HALO + SIDE, HALO : HALO + SIDE] = packed[...]
+    pump_cell, pump_tile = pumping(pump_rate, pump_well, owner_s, column_s, top_s)
+    wells = own_wells(owner, column, top, observed)
+    for copy in halo_copies:
+        copy.wait()
+    coefficients(ext, e_ref, r_ref, alpha_ref, beta_ref, pump_cell, pump_tile)
+    sweeps(e_ref, alpha_ref, beta_ref, u_ref, heads_ref)
+    residuals(heads_ref, wells, message, squares)
+    near_copies = [
+        remote(squares, near.at[i], near_send.at[i], near_recv.at[i], peer)
+        for i, peer in enumerate(near_peers)
+    ]
+    copies = [
+        remote(message, messages.at[8 - k], msg_send.at[k], msg_recv.at[k], neighbour(dx, dy))
+        for k, (dx, dy) in NEIGHBOURS
+    ]
+    messages[4] = message[...]
+    for copy in near_copies:
+        copy.wait()
+    here = squares[...]
+    for i in range(len(near_peers)):
+        here = here + near[i]
+    partial[...] = here
+    far_copies = [
+        remote(partial, far.at[i], far_send.at[i], far_recv.at[i], peer)
+        for i, peer in enumerate(far_peers)
+    ]
+    for copy in copies:
+        copy.wait()
     adjoint_source(messages, e_ref, r_ref, beta_ref, lhs)
     sweeps(e_ref, alpha_ref, beta_ref, u_ref, adjoint_ref)
-    scale = (-0.5 / (4 * TESTS_AXIS)) / (total[...] / WELLS + EPSILON)
+    for copy in far_copies:
+        copy.wait()
+    total = partial[...]
+    for i in range(len(far_peers)):
+        total = total + far[i]
+    scale = (-0.5 / (4 * TESTS_AXIS)) / (total / WELLS + EPSILON)
     sensitivity(e_ref, heads_ref, adjoint_ref, scale, sum_ref)
-    slabs(sum_ref, out)
-
-
-def reduce_kernel(parts, out, slots, send_sems, recv_sems):
-    me = lax.axis_index("test")
-    peers = [lax.rem(me + d, TESTS_AXIS) for d in range(1, TESTS_AXIS)]
-    greet([{"test": peer} for peer in peers])
-    copies = []
-    for i, peer in enumerate(peers):
-        copies.append(
-            pltpu.make_async_remote_copy(
-                src_ref=parts.at[peer],
-                dst_ref=slots.at[i],
-                send_sem=send_sems.at[i],
-                recv_sem=recv_sems.at[i],
-                device_id={"test": peer},
-                device_id_type=MESH,
-            )
-        )
-        copies[-1].start()
-    for copy in copies:
+    slabs(sum_ref, parts)
+    part_copies = [
+        remote(parts.at[peer], slots.at[i], part_send.at[i], part_recv.at[i], {"test": peer})
+        for i, peer in enumerate(test_peers)
+    ]
+    for copy in part_copies:
         copy.wait()
     total = parts[me]
     for i in range(TESTS_AXIS - 1):
@@ -419,21 +393,6 @@
             if xx:
                 plane = pltpu.roll(plane, 128 - 32 * xx, 1)
             out[4 * xq + xx] = plane[:, :32]
-
-
-def call(kernel, inputs, outputs, scratch, *args, collective_id=None):
-    remote = {} if collective_id is None else dict(collective_id=collective_id, has_side_effects=True)
-    specs = [pl.BlockSpec(memory_space=space) for space in inputs]
-    shapes = [jax.ShapeDtypeStruct(shape, F32) for shape in outputs]
-    out_specs = [pl.BlockSpec(memory_space=VMEM) for shape in outputs]
-    return pl.pallas_call(
-        kernel,
-        out_shape=shapes,
-        in_specs=specs,
-        out_specs=out_specs,
-        scratch_shapes=scratch,
-        compiler_params=pltpu.CompilerParams(vmem_limit_bytes=48 * 1024 * 1024, **remote),
-    )(*args)
 
 
 def local(
@@ -448,34 +407,23 @@
          jnp.zeros(shape, F32)],
         axis=2,
     )
-    (ext,) = call(
-        exchange_kernel, [VMEM], [field], [dma((9,)), dma((9,))], packed, collective_id=0
-    )
     table = [a.reshape(16, 128) for a in (owner, screen_column, screen_top)]
-    e, r, alpha, heads, message, squares = call(
-        heads_kernel, [VMEM] * 5 + [SMEM] * 5, [field] * 4 + [tile] * 2,
-        [VMEM(field, F32), VMEM(field, F32)],
-        ext, *table, observed, owner, screen_column, screen_top, pump_rate, pump_well,
-    )
     near, far = NX_BRICKS * ROUND - 1, NY_BRICKS // ROUND - 1
-    messages, total = call(
-        residual_exchange_kernel, [VMEM] * 2, [(9,) + tile, tile],
-        [VMEM((near,) + tile, F32), VMEM(tile, F32), VMEM((far,) + tile, F32),
-         dma((9,)), dma((9,)), dma((near,)), dma((near,)), dma((far,)), dma((far,))],
-        message, squares, collective_id=1,
-    )
-    (parts,) = call(
-        adjoint_kernel, [VMEM] * 6, [(TESTS_AXIS, 2) + tile],
-        [VMEM(field, F32), VMEM(field, F32), VMEM(field, F32), VMEM((SIDE, SIDE) + tile, F32),
-         VMEM((EXT - 2, (EXT - 2) * 8, 384), F32)],
-        e, r, alpha, heads, messages, total,
-    )
-    (gradient,) = call(
-        reduce_kernel, [VMEM], [(SIDE, SIDE, 32)],
-        [VMEM((TESTS_AXIS - 1, 2) + tile, F32), dma((TESTS_AXIS - 1,)), dma((TESTS_AXIS - 1,))],
-        parts, collective_id=2,
-    )
-    return gradient
+    scratch = [field] * 8 + [
+        (SIDE, SIDE) + tile, (EXT - 2, (EXT - 2) * 8, 384), tile, tile, (9,) + tile,
+        (near,) + tile, tile, (far,) + tile, (TESTS_AXIS, 2) + tile, (TESTS_AXIS - 1, 2) + tile,
+    ]
+    counts = (9, 9, 9, 9, near, near, far, far, TESTS_AXIS - 1, TESTS_AXIS - 1)
+    return pl.pallas_call(
+        kernel,
+        out_shape=jax.ShapeDtypeStruct((SIDE, SIDE, 32), F32),
+        in_specs=[pl.BlockSpec(memory_space=VMEM)] * 5 + [pl.BlockSpec(memory_space=SMEM)] * 5,
+        out_specs=pl.BlockSpec(memory_space=VMEM),
+        scratch_shapes=[VMEM(s, F32) for s in scratch] + [dma((n,)) for n in counts],
+        compiler_params=pltpu.CompilerParams(
+            vmem_limit_bytes=48 * 1024 * 1024, collective_id=0, has_side_effects=True
+        ),
+    )(packed, *table, observed, owner, screen_column, screen_top, pump_rate, pump_well)
 
 
 def solution(mesh):

time: 79.3 us -> 66.3 us (0.84)
  Pallas kernels: 76.2 us -> 62.7 us
    pallas_call x5 -> x1, Pallas kernels: 76.2 us -> 62.7 us  [local(): pl.pallas_call(kernel, out_shape=jax.ShapeDtypeStruct((SIDE, SIDE, 32), F...]
where the time goes in v2:
time: 66.3 us; the launch traced here: 66 us
  Pallas kernels  62.7 us (95%)
  local copies, waits for them, and re-layouts  3.09 us (5%)
    pallas_call x1, Pallas kernels, local(): pl.pallas_call(kernel, out_shape=jax.ShapeDtypeStruct((SIDE, SIDE, 32), F...  62.7 us
    unnamed x17, local copies, waits for them, and re-layouts  2.03 us

profile of v2, /device:TPU:1, one launch (start us, length us, event | category | flops | bytes accessed | tf_op | source)
XLA Modules:
  0.0 66.0 jit_solution(11860543859740722583)
XLA Ops:
  0.0 0.1 pad.3.clone
  0.1 0.0 copy-start.6
  0.1 0.9 %reshape.18 = f32[8,8,2,128]{3,2,1,0:T(2,128)S(1)} reshape(f32[8,8,256]{2,1,0:T(8,128)} %param.9) | data formatting | bytes 131072 | tf_op jit(solution)/shard_map/reshape | solution.py:406
  1.0 0.0 copy-done.6
  1.0 0.0 copy-start.7
  1.1 0.8 %copy-done.7 = f32[8,8,256]{2,1,0:T(8,128)S(1)} copy-done((f32[8,8,256]{2,1,0:T(8,128)S(1)}, f32[8,8,256]{2,1,0:T(8,128)}, u32[]{:S(2)}) %copy-start.7) | copy-done | bytes 65560
  1.9 0.0 copy-start
  1.9 0.0 copy-start.1
  1.9 0.0 copy-start.2
  1.9 0.0 copy-start.3
  1.9 0.0 copy-start.4
  1.9 0.0 copy-start.5
  2.0 0.1 maximum_maximum_fusion.packed
  2.1 0.6 copy-done
  2.6 0.0 copy-done.1
  2.6 0.0 copy-done.2
  2.6 0.0 copy-done.3
  2.7 0.0 copy-done.4
  2.7 0.0 copy-done.5
  2.7 62.7 %shard_map.91 = f32[8,8,32]{2,1,0:T(8,128)S(1)} custom-call(f32[8,8,8,128]{3,2,1,0:T(8,128)S(1)} %maximum_maximum_fusion.packed, s32[16,128]{1,0:T(8,128)S(1)} %bitcast.3, s32[16,128]{1,0:T(8,128)S(1)} %bitcast.4, s32[16,128]{1,0:T(8,128)S(1)} %bitcast.5, f32[4,2048]{1,0:T(4,128)S(1)} %copy-done, s32[2048]{0:T(1024)S(1)} %copy-done.1, s32[2048]{0:T(1024)S(1)} %copy-done.2, ...), custom_call_target="tpu_custom_call" | custom-call | tf_op jit(solution)/shard_map/pallas_call | solution.py:417
  65.4 0.6 copy.11
  (3 shorter events, 0.1 us)
Async XLA Ops:
  0.1 0.9 %copy-start.6 = (f32[8,8,256]{2,1,0:T(8,128)S(1)}, f32[8,8,256]{2,1,0:T(8,128)}, u32[]{:S(2)}) copy-start(f32[8,8,256]{2,1,0:T(8,128)} %param.10) | copy-start | bytes 196612
  1.0 0.8 %copy-start.7 = (f32[8,8,256]{2,1,0:T(8,128)S(1)}, f32[8,8,256]{2,1,0:T(8,128)}, u32[]{:S(2)}) copy-start(f32[8,8,256]{2,1,0:T(8,128)} %param.11) | copy-start | bytes 196612
  1.9 0.8 %copy-start = (f32[4,2048]{1,0:T(4,128)S(1)}, f32[4,2048]{1,0:T(4,128)}, u32[]{:S(2)}) copy-start(f32[4,2048]{1,0:T(4,128)} %observed.1) | copy-start | bytes 98308
  1.9 0.8 %copy-start.1 = (s32[2048]{0:T(1024)S(1)}, s32[2048]{0:T(1024)}, u32[]{:S(2)}) copy-start(s32[2048]{0:T(1024)} %owner_s.1) | copy-start | bytes 24580
  1.9 0.7 %copy-start.2 = (s32[2048]{0:T(1024)S(1)}, s32[2048]{0:T(1024)}, u32[]{:S(2)}) copy-start(s32[2048]{0:T(1024)} %column_s.1) | copy-start | bytes 24580
  1.9 0.7 %copy-start.3 = (s32[2048]{0:T(1024)S(1)}, s32[2048]{0:T(1024)}, u32[]{:S(2)}) copy-start(s32[2048]{0:T(1024)} %top_s.1) | copy-start | bytes 24580
  1.9 0.7 %copy-start.4 = (f32[4]{0:T(128)S(1)}, f32[4]{0:T(128)}, u32[]{:S(2)}) copy-start(f32[4]{0:T(128)} %pump_rate.1) | copy-start | bytes 52
  1.9 0.7 %copy-start.5 = (s32[4]{0:T(128)S(1)}, s32[4]{0:T(128)}, u32[]{:S(2)}) copy-start(s32[4]{0:T(128)} %pump_well.1) | copy-start | bytes 52

commit v3 on v2

--- a/solution.py
+++ b/solution.py
@@ -78,14 +78,6 @@
     }
 
 
-def span(step, width):
-    if step == 0:
-        return 0, HALO, SIDE
-    if step > 0:
-        return SIDE - width, HALO - width, width
-    return 0, HALO + SIDE, width
-
-
 def remote(source, target, send_sem, recv_sem, peer):
     copy = pltpu.make_async_remote_copy(
         src_ref=source, dst_ref=target, send_sem=send_sem, recv_sem=recv_sem,
@@ -95,20 +87,47 @@
     return copy
 
 
-def start_halos(packed, ext, send_sems, recv_sems):
-    copies = []
-    for k, (dx, dy) in NEIGHBOURS:
-        width = HALO if dx == 0 or dy == 0 else HALO - 1
-        from_x, to_x, count_x = span(dx, width)
-        from_y, to_y, count_y = span(dy, width)
-        copies.append(
-            remote(
-                packed.at[pl.ds(from_x, count_x), pl.ds(from_y, count_y)],
-                ext.at[pl.ds(to_x, count_x), pl.ds(to_y, count_y)],
-                send_sems.at[k], recv_sems.at[k], neighbour(dx, dy),
-            )
-        )
-    return copies
+def halo_copies(packed, ext, send_sems, recv_sems):
+    me = lax.axis_index("test")
+    core = lax.rem(me, 2)
+    partner = {"test": me + 1 - 2 * core}
+    deep = HALO - 1
+    first, second = [], []
+    half = pl.ds(SIDE // 2 * core, SIDE // 2)
+    half_there = pl.ds(HALO + SIDE // 2 * core, SIDE // 2)
+    corner = pl.ds((SIDE - deep) * core, deep)
+    corner_there = pl.ds((HALO + SIDE) * (1 - core) + core, deep)
+    for dy, from_y, to_y, skip in ((1, SIDE - deep, 1, 1), (-1, 0, HALO + SIDE, 0)):
+        first.append(
+            (half, pl.ds(from_y, deep), half_there, pl.ds(to_y, deep), neighbour(0, dy))
+        )
+        first.append(
+            (corner, pl.ds(from_y + skip, deep - 1), corner_there, pl.ds(to_y + skip, deep - 1),
+             neighbour(2 * core - 1, dy))
+        )
+    first = [first[0], first[2], first[1], first[3]]
+    for dx, from_x, to_x in ((1, SIDE - HALO, 0), (-1, 0, HALO + SIDE)):
+        second.append(
+            (pl.ds(from_x, HALO), pl.ds(0, SIDE), pl.ds(to_x, HALO), pl.ds(HALO, SIDE),
+             neighbour(dx, 0))
+        )
+    started = [
+        remote(packed.at[x, y], ext.at[to_x, to_y], send_sems.at[k], recv_sems.at[k], peer)
+        for k, (x, y, to_x, to_y, peer) in enumerate(first + second)
+    ]
+
+    def finish():
+        passed = []
+        for k, (x, y, to_x, to_y, peer) in enumerate(first):
+            started[k].wait_recv()
+            block = ext.at[to_x, to_y]
+            passed.append(remote(block, block, send_sems.at[6 + k], recv_sems.at[6 + k], partner))
+        for copy in started[: len(first)]:
+            copy.wait_send()
+        for copy in started[len(first) :] + passed:
+            copy.wait()
+
+    return finish
 
 
 def coefficients(ext, e_ref, r_ref, alpha_ref, beta_ref, pump_cell, pump_tile):
@@ -117,6 +136,26 @@
 
     rows(0, EXT, roots)
     lo, hi = 1, EXT - 1
+
+    def edge(xs, y, source_y):
+        count = xs.stop - xs.start
+        shape = (count, 8, 128)
+        first = ext[xs, source_y, 6:7, :]
+        second = ext[xs, source_y, 7:8, :]
+        logs = jnp.where(
+            iota(shape, 1) < 4, jnp.broadcast_to(first, shape), jnp.broadcast_to(second, shape)
+        )
+        gx = lax.axis_index("bx") * SIDE + xs.start - HALO + iota(shape, 0)
+        gy = lax.axis_index("by") * SIDE + y - HALO + jnp.zeros(shape, jnp.int32)
+        ok = (gx >= 0) & (gx < NX_BRICKS * SIDE) & (gy >= 0) & (gy < NY_BRICKS * SIDE)
+        e_ref[xs, y] = jnp.where(ok, jnp.exp(0.5 * logs), 1.0)
+
+    middle = slice(HALO, HALO + SIDE)
+    edge(middle, 0, 1)
+    edge(middle, EXT - 1, EXT - 2)
+    for x in (HALO - 1, HALO + SIDE):
+        edge(slice(x, x + 1), 1, 2)
+        edge(slice(x, x + 1), EXT - 2, EXT - 3)
 
     def terms(x):
         e = e_ref[x, lo:hi]
@@ -338,12 +377,11 @@
     for peer in everyone:
         pl.semaphore_signal(barrier, inc=1, device_id=peer, device_id_type=MESH)
     pl.semaphore_wait(barrier, len(everyone))
-    halo_copies = start_halos(packed, ext, halo_send, halo_recv)
+    finish_halo = halo_copies(packed, ext, halo_send, halo_recv)
     ext[HALO : HALO + SIDE, HALO : HALO + SIDE] = packed[...]
     pump_cell, pump_tile = pumping(pump_rate, pump_well, owner_s, column_s, top_s)
     wells = own_wells(owner, column, top, observed)
-    for copy in halo_copies:
-        copy.wait()
+    finish_halo()
     coefficients(ext, e_ref, r_ref, alpha_ref, beta_ref, pump_cell, pump_tile)
     sweeps(e_ref, alpha_ref, beta_ref, u_ref, heads_ref)
     residuals(heads_ref, wells, message, squares)
@@ -402,10 +440,9 @@
     field = (EXT, EXT, 8, 128)
     tile = (8, 128)
     shape = (SIDE, SIDE, 2, 128)
+    further = jnp.concatenate([log_conductivity[:, 1:5], log_conductivity[:, 3:7]], axis=1)
     packed = jnp.concatenate(
-        [log_conductivity.reshape(shape), storage.reshape(shape), recharge.reshape(shape),
-         jnp.zeros(shape, F32)],
-        axis=2,
+        [a.reshape(shape) for a in (log_conductivity, storage, recharge, further)], axis=2
     )
     table = [a.reshape(16, 128) for a in (owner, screen_column, screen_top)]
     near, far = NX_BRICKS * ROUND - 1, NY_BRICKS // ROUND - 1
@@ -413,7 +450,7 @@
         (SIDE, SIDE) + tile, (EXT - 2, (EXT - 2) * 8, 384), tile, tile, (9,) + tile,
         (near,) + tile, tile, (far,) + tile, (TESTS_AXIS, 2) + tile, (TESTS_AXIS - 1, 2) + tile,
     ]
-    counts = (9, 9, 9, 9, near, near, far, far, TESTS_AXIS - 1, TESTS_AXIS - 1)
+    counts = (10, 10, 9, 9, near, near, far, far, TESTS_AXIS - 1, TESTS_AXIS - 1)
     return pl.pallas_call(
         kernel,
         out_shape=jax.ShapeDtypeStruct((SIDE, SIDE, 32), F32),

time: 66.3 us -> 56.6 us (0.85)
  Pallas kernels: 62.7 us -> 53 us
    pallas_call x1, Pallas kernels: 62.7 us -> 53 us  [local(): pl.pallas_call(kernel, out_shape=jax.ShapeDtypeStruct((SIDE, SIDE, 32), F...]
where the time goes in v3:
time: 56.6 us; the launch traced here: 56.3 us
  Pallas kernels  53 us (94%)
  local copies, waits for them, and re-layouts  3.03 us (5%)
    pallas_call x1, Pallas kernels, local(): pl.pallas_call(kernel, out_shape=jax.ShapeDtypeStruct((SIDE, SIDE, 32), F...  53 us
    unnamed x17, local copies, waits for them, and re-layouts  2.01 us

profile of v3, /device:TPU:1, one launch (start us, length us, event | category | flops | bytes accessed | tf_op | source)
XLA Modules:
  0.0 56.3 jit_solution(5910162050852176654)
XLA Ops:
  0.0 0.0 copy-start.7
  0.0 0.9 %reshape.22 = f32[8,8,2,128]{3,2,1,0:T(2,128)S(1)} reshape(f32[8,8,256]{2,1,0:T(8,128)} %param.10) | data formatting | bytes 131072 | tf_op jit(solution)/shard_map/reshape | solution.py:445
  0.9 0.0 copy-done.7
  0.9 0.0 copy-start.6
  1.0 0.8 %copy-done.6 = f32[8,8,256]{2,1,0:T(8,128)S(1)} copy-done((f32[8,8,256]{2,1,0:T(8,128)S(1)}, f32[8,8,256]{2,1,0:T(8,128)}, u32[]{:S(2)}) %copy-start.6) | copy-done | bytes 65560
  1.9 0.0 copy-start
  1.9 0.0 copy-start.1
  1.9 0.0 copy-start.2
  1.9 0.0 copy-start.3
  1.9 0.0 copy-start.4
  2.0 0.0 copy-start.5
  2.0 0.1 pad_maximum_fusion.packed
  2.1 0.6 copy-done
  2.7 0.0 copy-done.1
  2.7 0.0 copy-done.2
  2.7 0.0 copy-done.3
  2.7 0.0 copy-done.4
  2.7 0.0 copy-done.5
  2.7 53.0 %shard_map.91 = f32[8,8,32]{2,1,0:T(8,128)S(1)} custom-call(f32[8,8,8,128]{3,2,1,0:T(8,128)S(1)} %pad_maximum_fusion.packed, s32[16,128]{1,0:T(8,128)S(1)} %bitcast.3, s32[16,128]{1,0:T(8,128)S(1)} %bitcast.4, s32[16,128]{1,0:T(8,128)S(1)} %bitcast.5, f32[4,2048]{1,0:T(4,128)S(1)} %copy-done, s32[2048]{0:T(1024)S(1)} %copy-done.1, s32[2048]{0:T(1024)S(1)} %copy-done.2, ...), custom_call_target="tpu_custom_call" | custom-call | tf_op jit(solution)/shard_map/pallas_call | solution.py:454
  55.7 0.6 %copy.11 = f32[8,8,32]{2,1,0:T(8,128)} copy(f32[8,8,32]{2,1,0:T(8,128)S(1)} %shard_map.91) | data formatting | bytes 16384
  (5 shorter events, 0.1 us)
Async XLA Ops:
  0.0 0.9 %copy-start.7 = (f32[8,8,256]{2,1,0:T(8,128)S(1)}, f32[8,8,256]{2,1,0:T(8,128)}, u32[]{:S(2)}) copy-start(f32[8,8,256]{2,1,0:T(8,128)} %param.11) | copy-start | bytes 196612
  0.9 0.8 %copy-start.6 = (f32[8,8,256]{2,1,0:T(8,128)S(1)}, f32[8,8,256]{2,1,0:T(8,128)}, u32[]{:S(2)}) copy-start(f32[8,8,256]{2,1,0:T(8,128)} %param.9) | copy-start | bytes 196612
  1.9 0.8 %copy-start = (f32[4,2048]{1,0:T(4,128)S(1)}, f32[4,2048]{1,0:T(4,128)}, u32[]{:S(2)}) copy-start(f32[4,2048]{1,0:T(4,128)} %observed.1) | copy-start | bytes 98308
  1.9 0.8 %copy-start.1 = (s32[2048]{0:T(1024)S(1)}, s32[2048]{0:T(1024)}, u32[]{:S(2)}) copy-start(s32[2048]{0:T(1024)} %owner_s.1) | copy-start | bytes 24580
  1.9 0.7 %copy-start.2 = (s32[2048]{0:T(1024)S(1)}, s32[2048]{0:T(1024)}, u32[]{:S(2)}) copy-start(s32[2048]{0:T(1024)} %column_s.1) | copy-start | bytes 24580
  1.9 0.7 %copy-start.3 = (s32[2048]{0:T(1024)S(1)}, s32[2048]{0:T(1024)}, u32[]{:S(2)}) copy-start(s32[2048]{0:T(1024)} %top_s.1) | copy-start | bytes 24580
  1.9 0.7 %copy-start.4 = (f32[4]{0:T(128)S(1)}, f32[4]{0:T(128)}, u32[]{:S(2)}) copy-start(f32[4]{0:T(128)} %pump_rate.1) | copy-start | bytes 52
  2.0 0.7 %copy-start.5 = (s32[4]{0:T(128)S(1)}, s32[4]{0:T(128)}, u32[]{:S(2)}) copy-start(s32[4]{0:T(128)} %pump_well.1) | copy-start | bytes 52

commit v4 on v3

--- a/solution.py
+++ b/solution.py
@@ -8,7 +8,6 @@
 F32 = jnp.float32
 MESH = pl.DeviceIdType.MESH
 VMEM = pltpu.VMEM
-SMEM = pltpu.SMEM
 HIGHEST = lax.Precision.HIGHEST
 EPSILON = 1e-06
 SCREEN = 8
@@ -20,7 +19,9 @@
 TESTS_AXIS = 8
 WELLS = 2048
 OWN = 32
+GROUPS = 7
 DIRECTIONS = [(dx, dy) for dx in (-1, 0, 1) for dy in (-1, 0, 1)]
+FACES = [(1, 0), (-1, 0), (0, 1), (0, -1)]
 NEIGHBOURS = [(k, d) for k, d in enumerate(DIRECTIONS) if d != (0, 0)]
 
 
@@ -46,12 +47,21 @@
     )
 
 
-def rows(lo, hi, body):
-    def step(x, carry):
-        body(x)
+def rows(lo, hi, body, group):
+    def step(i, carry):
+        for j in range(group):
+            body(lo + i * group + j)
         return carry
 
-    lax.fori_loop(lo, hi, step, 0)
+    lax.fori_loop(0, (hi - lo) // group, step, 0)
+
+
+def thirds(values):
+    parts, rest = [], values
+    for i in range(3):
+        parts.append(rest.astype(jnp.bfloat16))
+        rest = rest - parts[-1].astype(F32)
+    return parts
 
 
 def halves(ref, x, lo, hi, field):
@@ -134,7 +144,7 @@
     def roots(x):
         e_ref[x] = jnp.where(inside(x, 0, EXT), jnp.exp(0.5 * halves(ext, x, 0, EXT, 0)), 1.0)
 
-    rows(0, EXT, roots)
+    rows(0, EXT, roots, 4)
     lo, hi = 1, EXT - 1
 
     def edge(xs, y, source_y):
@@ -168,7 +178,7 @@
         alpha_ref[x, lo:hi] = e * er
         beta_ref[x, lo:hi] = er * source
 
-    rows(lo, hi, terms)
+    rows(lo, hi, terms, 2)
 
 
 def sweeps(e_ref, alpha_ref, beta_ref, u_ref, out_ref):
@@ -177,13 +187,13 @@
             beta_ref, x, 2, EXT - 2, 0.0
         )
 
-    rows(2, EXT - 2, second)
+    rows(2, EXT - 2, second, 4)
 
     def third(x):
         u = beta_ref[x, 3 : EXT - 3] + alpha_ref[x, 3 : EXT - 3] * around(u_ref, x, 3, EXT - 3, 0.0)
         out_ref[x, 3 : EXT - 3] = u / e_ref[x, 3 : EXT - 3]
 
-    rows(3, EXT - 3, third)
+    rows(3, EXT - 3, third, 5)
 
 
 def pumping(pump_rate, pump_well, owner, column, top):
@@ -193,17 +203,35 @@
     tile = jnp.zeros((8, 128), F32)
     first_x = lax.axis_index("bx") * SIDE - HALO
     first_y = lax.axis_index("by") * SIDE - HALO
+    code = (owner[...] * 64 + column[...]) * 256 + top[...]
+    code = code.astype(F32)
+    index = iota((16, 128), 0) * 128 + iota((16, 128), 1)
     for t in range(4):
-        well = pump_well[t]
-        brick, place, start = owner[well], column[well], top[well]
+        well = jnp.broadcast_to(pump_well[0:1, t : t + 1], (16, 128))
+        found = jnp.sum(jnp.where(index == well, code, 0.0), axis=0, keepdims=True)
+        found = jnp.broadcast_to(jnp.sum(found, axis=1, keepdims=True), (8, 128)).astype(jnp.int32)
+        brick, place, start = found >> 14, (found >> 8) & 63, found & 255
         x = (brick >> 4) * SIDE + (place >> 3) - first_x
         y = (brick & 15) * SIDE + (place & 7) - first_y
         ok = (x >= 0) & (x < EXT) & (y >= 0) & (y < EXT)
         mine = (sub & 3) == t
         cell = jnp.where(mine, jnp.where(ok, x * EXT + y, -1), cell)
         hit = mine & (z >= start) & (z < start + SCREEN)
-        tile = jnp.where(hit, -pump_rate[t], tile)
+        tile = jnp.where(hit, -jnp.broadcast_to(pump_rate[0:1, t : t + 1], (8, 128)), tile)
     return cell, tile
+
+
+def pack(log_conductivity, storage, recharge, packed):
+    def row(x):
+        logs = log_conductivity[x]
+        further = jnp.where(
+            iota((SIDE, 256), 0) < 4, pltpu.roll(logs, SIDE - 1, 0), pltpu.roll(logs, 1, 0)
+        )
+        for field, values in enumerate((logs, storage[x], recharge[x], further)):
+            packed[x, :, 2 * field, :] = values[:, :128]
+            packed[x, :, 2 * field + 1, :] = values[:, 128:]
+
+    rows(0, SIDE, row, 2)
 
 
 def own_wells(owner, column, top, observed):
@@ -236,8 +264,10 @@
     z = (iota((2 * OWN, 128), 1) + 128 * half).astype(F32)
     screen = jnp.where((z >= top2) & (z < top2 + SCREEN), 1.0, 0.0)
     heads = heads_ref[HALO : HALO + SIDE, HALO : HALO + SIDE].reshape(512, 128)
+    screen = screen.astype(jnp.bfloat16)
     sums = lax.dot_general(
-        screen, heads, (((1,), (1,)), ((), ())), precision=HIGHEST, preferred_element_type=F32
+        jnp.concatenate([screen] * 3, axis=1), jnp.concatenate(thirds(heads), axis=1),
+        (((1,), (1,)), ((), ())), preferred_element_type=F32,
     )
     at = iota((2 * OWN, 512), 1)
     keep = ((at >> 3).astype(F32) == column2) & (
@@ -245,7 +275,8 @@
     )
     sums = jnp.where(keep, sums, 0.0)
     pick = jnp.where((iota((512, 128), 0) & 3) == iota((512, 128), 1), 1.0, 0.0)
-    sums = jnp.dot(sums, pick, precision=HIGHEST, preferred_element_type=F32)
+    pick = pick.astype(jnp.bfloat16)
+    sums = sum(jnp.dot(part, pick, preferred_element_type=F32) for part in thirds(sums))
     sums = (sums[:OWN] + sums[OWN:]) * (1.0 / SCREEN)
     lane = iota((OWN, 128), 1)
     for t in range(4):
@@ -263,9 +294,9 @@
 
 def adjoint_source(messages, e_ref, r_ref, beta_ref, lhs):
     sub, lane = iota((8, 128), 0), iota((8, 128), 1)
-    values = [jnp.zeros((8, 128), F32) for g in range(3)]
-    cells = [jnp.zeros((8, 128), F32) for g in range(3)]
-    tops = [jnp.zeros((8, 128), F32) for g in range(3)]
+    values = [jnp.zeros((8, 128), F32) for g in range(GROUPS)]
+    cells = [jnp.zeros((8, 128), F32) for g in range(GROUPS)]
+    tops = [jnp.zeros((8, 128), F32) for g in range(GROUPS)]
     for k, (dx, dy) in enumerate(DIRECTIONS):
         tile = messages[k]
         value = jnp.where(sub < 4, tile, pltpu.roll(tile, 4, 0))
@@ -276,15 +307,17 @@
         ok = (x >= 1) & (x < EXT - 1) & (y >= 1) & (y < EXT - 1) & (lane < OWN)
         cell = jnp.where(ok, x * EXT + y, 0.0)
         top = jnp.where(lane < OWN, jnp.broadcast_to(tile[5:6], (8, 128)), 0.0)
-        g, shift = k // 4, OWN * (k % 4)
-        if shift:
-            value, cell, top = [pltpu.roll(v, shift, 1) for v in (value, cell, top)]
-        values[g], cells[g], tops[g] = values[g] + value, cells[g] + cell, tops[g] + top
+        for p, part in enumerate(thirds(value)):
+            g, shift = (3 * k + p) // 4, OWN * ((3 * k + p) % 4)
+            moved = [part.astype(F32), cell, top]
+            if shift:
+                moved = [pltpu.roll(v, shift, 1) for v in moved]
+            values[g], cells[g], tops[g] = values[g] + moved[0], cells[g] + moved[1], tops[g] + moved[2]
     z = iota((256, 128), 0).astype(F32)
     screens = []
-    for g in range(3):
+    for g in range(GROUPS):
         top = jnp.broadcast_to(tops[g][0:1], (256, 128))
-        screens.append(jnp.where((z >= top) & (z < top + SCREEN), 1.0, 0.0))
+        screens.append(jnp.where((z >= top) & (z < top + SCREEN), 1.0, 0.0).astype(jnp.bfloat16))
     screen = jnp.concatenate(screens, axis=1)
     wide = EXT - 2
     shape = (wide, 8, 128)
@@ -292,17 +325,19 @@
 
     def left(x):
         cell = (x * EXT + 1 + iota(shape, 0)).astype(F32)
-        for g in range(3):
-            lhs[x - 1, :, g * 128 : (g + 1) * 128] = jnp.where(
-                cells[g][None] == cell, values[g][None], 0.0
-            ).reshape(wide * 8, 128)
-
-    rows(lo, hi, left)
+        for g in range(GROUPS):
+            lhs[x - 1, :, g * 128 : (g + 1) * 128] = (
+                jnp.where(cells[g][None] == cell, values[g][None], 0.0)
+                .reshape(wide * 8, 128)
+                .astype(jnp.bfloat16)
+            )
+
+    rows(lo, hi, left, 2)
     group = 7
     for first in range(0, wide, group):
-        block = lhs[first : first + group].reshape(group * wide * 8, 384)
+        block = lhs[first : first + group].reshape(group * wide * 8, GROUPS * 128)
         both = lax.dot_general(
-            block, screen, (((1,), (1,)), ((), ())), precision=HIGHEST, preferred_element_type=F32
+            block, screen, (((1,), (1,)), ((), ())), preferred_element_type=F32
         )
         pair = both.reshape(group, wide, 8, 256)
         for i in range(group):
@@ -311,25 +346,37 @@
             beta_ref[x, lo:hi] = e_ref[x, lo:hi] * r_ref[x, lo:hi] * source
 
 
-def sensitivity(e_ref, heads_ref, adjoint_ref, scale, out_ref):
+def head_steps(e_ref, heads_ref, steps_ref):
     lo, hi = HALO, HALO + SIDE
 
-    def cell_terms(x):
-        h, a = heads_ref[x, lo:hi], adjoint_ref[x, lo:hi]
-        e = e_ref[x, lo:hi]
-        total = jnp.zeros_like(h)
-        for step_x, step_y in ((1, 0), (-1, 0), (0, 1), (0, -1)):
+    def row(x):
+        h, e = heads_ref[x, lo:hi], e_ref[x, lo:hi]
+        for f, (step_x, step_y) in enumerate(FACES):
             at = (x + step_x, slice(lo + step_y, hi + step_y))
-            total = total + e_ref[at] * (h - heads_ref[at]) * (a - adjoint_ref[at])
-        for e_n, h_n, a_n in zip(
-            z_neighbours(e, 1.0), z_neighbours(h, 0.0), z_neighbours(a, 0.0)
-        ):
-            total = total + e_n * (h - h_n) * (a - a_n)
-        total = total * e * scale[None]
+            steps_ref[f, x - HALO] = e * e_ref[at] * (h - heads_ref[at])
+        for f, (e_n, h_n) in enumerate(zip(z_neighbours(e, 1.0), z_neighbours(h, 0.0))):
+            steps_ref[4 + f, x - HALO] = e * e_n * (h - h_n)
+
+    rows(lo, hi, row, 2)
+
+
+def sensitivity(steps_ref, adjoint_ref, scale, out_ref):
+    lo, hi = HALO, HALO + SIDE
+
+    def row(x):
+        a = adjoint_ref[x, lo:hi]
+        total = jnp.zeros_like(a)
+        for f, (step_x, step_y) in enumerate(FACES):
+            total = total + steps_ref[f, x - HALO] * (
+                a - adjoint_ref[x + step_x, lo + step_y : hi + step_y]
+            )
+        for f, a_n in enumerate(z_neighbours(a, 0.0)):
+            total = total + steps_ref[4 + f, x - HALO] * (a - a_n)
+        total = total * scale[None]
         total = total + pltpu.roll(total, 7, 1)
         out_ref[x - HALO] = total + pltpu.roll(total, 6, 1)
 
-    rows(lo, hi, cell_terms)
+    rows(lo, hi, row, 4)
 
 
 def slabs(sum_ref, out):
@@ -349,8 +396,8 @@
 
 
 def kernel(
-    packed, owner, column, top, observed, owner_s, column_s, top_s, pump_rate, pump_well, out,
-    ext, e_ref, r_ref, alpha_ref, heads_ref, beta_ref, u_ref, adjoint_ref, sum_ref, lhs,
+    log_conductivity, storage, recharge, owner, column, top, observed, pump_rate, pump_well, out,
+    packed, steps_ref, lhs, ext, e_ref, r_ref, alpha_ref, heads_ref, beta_ref, u_ref, adjoint_ref, sum_ref,
     message, squares, messages, near, partial, far, parts, slots,
     halo_send, halo_recv, msg_send, msg_recv, near_send, near_recv, far_send, far_recv,
     part_send, part_recv,
@@ -376,10 +423,11 @@
     barrier = pltpu.get_barrier_semaphore()
     for peer in everyone:
         pl.semaphore_signal(barrier, inc=1, device_id=peer, device_id_type=MESH)
+    pack(log_conductivity, storage, recharge, packed)
     pl.semaphore_wait(barrier, len(everyone))
     finish_halo = halo_copies(packed, ext, halo_send, halo_recv)
     ext[HALO : HALO + SIDE, HALO : HALO + SIDE] = packed[...]
-    pump_cell, pump_tile = pumping(pump_rate, pump_well, owner_s, column_s, top_s)
+    pump_cell, pump_tile = pumping(pump_rate, pump_well, owner, column, top)
     wells = own_wells(owner, column, top, observed)
     finish_halo()
     coefficients(ext, e_ref, r_ref, alpha_ref, beta_ref, pump_cell, pump_tile)
@@ -404,6 +452,7 @@
         remote(partial, far.at[i], far_send.at[i], far_recv.at[i], peer)
         for i, peer in enumerate(far_peers)
     ]
+    head_steps(e_ref, heads_ref, steps_ref)
     for copy in copies:
         copy.wait()
     adjoint_source(messages, e_ref, r_ref, beta_ref, lhs)
@@ -414,7 +463,7 @@
     for i in range(len(far_peers)):
         total = total + far[i]
     scale = (-0.5 / (4 * TESTS_AXIS)) / (total / WELLS + EPSILON)
-    sensitivity(e_ref, heads_ref, adjoint_ref, scale, sum_ref)
+    sensitivity(steps_ref, adjoint_ref, scale, sum_ref)
     slabs(sum_ref, parts)
     part_copies = [
         remote(parts.at[peer], slots.at[i], part_send.at[i], part_recv.at[i], {"test": peer})
@@ -439,28 +488,31 @@
     dma = pltpu.SemaphoreType.DMA
     field = (EXT, EXT, 8, 128)
     tile = (8, 128)
-    shape = (SIDE, SIDE, 2, 128)
-    further = jnp.concatenate([log_conductivity[:, 1:5], log_conductivity[:, 3:7]], axis=1)
-    packed = jnp.concatenate(
-        [a.reshape(shape) for a in (log_conductivity, storage, recharge, further)], axis=2
-    )
     table = [a.reshape(16, 128) for a in (owner, screen_column, screen_top)]
     near, far = NX_BRICKS * ROUND - 1, NY_BRICKS // ROUND - 1
     scratch = [field] * 8 + [
-        (SIDE, SIDE) + tile, (EXT - 2, (EXT - 2) * 8, 384), tile, tile, (9,) + tile,
+        (SIDE, SIDE) + tile, tile, tile, (9,) + tile,
         (near,) + tile, tile, (far,) + tile, (TESTS_AXIS, 2) + tile, (TESTS_AXIS - 1, 2) + tile,
     ]
     counts = (10, 10, 9, 9, near, near, far, far, TESTS_AXIS - 1, TESTS_AXIS - 1)
     return pl.pallas_call(
         kernel,
         out_shape=jax.ShapeDtypeStruct((SIDE, SIDE, 32), F32),
-        in_specs=[pl.BlockSpec(memory_space=VMEM)] * 5 + [pl.BlockSpec(memory_space=SMEM)] * 5,
+        in_specs=[pl.BlockSpec(memory_space=VMEM)] * 9,
         out_specs=pl.BlockSpec(memory_space=VMEM),
-        scratch_shapes=[VMEM(s, F32) for s in scratch] + [dma((n,)) for n in counts],
+        scratch_shapes=[
+            VMEM((SIDE, SIDE) + tile, F32),
+            VMEM((6, SIDE, SIDE) + tile, F32),
+            VMEM((EXT - 2, (EXT - 2) * 8, GROUPS * 128), jnp.bfloat16),
+        ]
+        + [VMEM(s, F32) for s in scratch] + [dma((n,)) for n in counts],
         compiler_params=pltpu.CompilerParams(
             vmem_limit_bytes=48 * 1024 * 1024, collective_id=0, has_side_effects=True
         ),
-    )(packed, *table, observed, owner, screen_column, screen_top, pump_rate, pump_well)
+    )(
+        log_conductivity, storage, recharge, *table, observed,
+        pump_rate.reshape(1, 4), pump_well.reshape(1, 4),
+    )
 
 
 def solution(mesh):

time: 56.6 us -> 55.9 us (0.988)
  Pallas kernels: 53 us -> 49.4 us
  local copies, waits for them, and re-layouts: 3.03 us -> 5.98 us
    unnamed x17 -> x19, local copies, waits for them, and re-layouts: 2.01 us -> 5.98 us
    pallas_call x1, Pallas kernels: 53 us -> 49.4 us  [local(): pl.pallas_call(kernel, out_shape=jax.ShapeDtypeStruct((SIDE, SIDE, 32), F...]
    reshape x4 -> x0, local copies, waits for them, and re-layouts: 1.01 us -> none  [local(): a.reshape(shape)]
where the time goes in v4:
time: 55.9 us; the launch traced here: 55.4 us
  Pallas kernels  49.4 us (88%)
  local copies, waits for them, and re-layouts  5.98 us (11%)
    pallas_call x1, Pallas kernels, local(): pl.pallas_call(kernel, out_shape=jax.ShapeDtypeStruct((SIDE, SIDE, 32), F...  49.4 us
    unnamed x19, local copies, waits for them, and re-layouts  5.98 us

profile of v4, /device:TPU:1, one launch (start us, length us, event | category | flops | bytes accessed | tf_op | source)
XLA Modules:
  0.0 55.4 jit_solution(2636647800650192409)
XLA Ops:
  0.0 0.0 copy-start.4
  0.0 0.0 copy-start.7
  0.0 0.0 copy-start.8
  0.0 0.7 %copy-done.4 = s32[2048]{0:T(1024)S(1)} copy-done((s32[2048]{0:T(1024)S(1)}, s32[2048]{0:T(1024)}, u32[]{:S(2)}) %copy-start.4) | copy-done | bytes 8216
  0.7 0.0 copy-done.7
  0.7 0.0 copy-done.8
  0.7 0.0 copy-start
  0.7 0.8 %copy-done = f32[8,8,256]{2,1,0:T(8,128)S(1)} copy-done((f32[8,8,256]{2,1,0:T(8,128)S(1)}, f32[8,8,256]{2,1,0:T(8,128)}, u32[]{:S(2)}) %copy-start) | copy-done | bytes 65560
  1.5 0.0 copy-start.1
  1.5 0.8 %copy-done.1 = f32[8,8,256]{2,1,0:T(8,128)S(1)} copy-done((f32[8,8,256]{2,1,0:T(8,128)S(1)}, f32[8,8,256]{2,1,0:T(8,128)}, u32[]{:S(2)}) %copy-start.1) | copy-done | bytes 65560
  2.4 0.0 copy-start.2
  2.4 0.8 %copy-done.2 = f32[8,8,256]{2,1,0:T(8,128)S(1)} copy-done((f32[8,8,256]{2,1,0:T(8,128)S(1)}, f32[8,8,256]{2,1,0:T(8,128)}, u32[]{:S(2)}) %copy-start.2) | copy-done | bytes 65560
  3.2 0.0 copy-start.3
  3.2 0.8 %copy-done.3 = f32[4,2048]{1,0:T(4,128)S(1)} copy-done((f32[4,2048]{1,0:T(4,128)S(1)}, f32[4,2048]{1,0:T(4,128)}, u32[]{:S(2)}) %copy-start.3) | copy-done | bytes 32792
  4.0 0.0 copy-start.5
  4.0 0.7 %copy-done.5 = s32[2048]{0:T(1024)S(1)} copy-done((s32[2048]{0:T(1024)S(1)}, s32[2048]{0:T(1024)}, u32[]{:S(2)}) %copy-start.5) | copy-done | bytes 8216
  4.7 0.0 copy-start.6
  4.7 0.7 %copy-done.6 = s32[2048]{0:T(1024)S(1)} copy-done((s32[2048]{0:T(1024)S(1)}, s32[2048]{0:T(1024)}, u32[]{:S(2)}) %copy-start.6) | copy-done | bytes 8216
  5.4 49.4 %shard_map.91 = f32[8,8,32]{2,1,0:T(8,128)S(1)} custom-call(f32[8,8,256]{2,1,0:T(8,128)S(1)} %copy-done, f32[8,8,256]{2,1,0:T(8,128)S(1)} %copy-done.1, f32[8,8,256]{2,1,0:T(8,128)S(1)} %copy-done.2, s32[16,128]{1,0:T(8,128)S(1)} %bitcast.5, s32[16,128]{1,0:T(8,128)S(1)} %bitcast.6, s32[16,128]{1,0:T(8,128)S(1)} %bitcast.7, f32[4,2048]{1,0:T(4,128)S(1)} %copy-done.3, ...), custom_call_target="tpu_custom_call" | custom-call | tf_op jit(solution)/shard_map/pallas_call | solution.py:498
  54.8 0.6 %copy.11 = f32[8,8,32]{2,1,0:T(8,128)} copy(f32[8,8,32]{2,1,0:T(8,128)S(1)} %shard_map.91) | data formatting | bytes 16384
Async XLA Ops:
  0.0 0.7 %copy-start.4 = (s32[2048]{0:T(1024)S(1)}, s32[2048]{0:T(1024)}, u32[]{:S(2)}) copy-start(s32[2048]{0:T(1024)} %param.15) | copy-start | bytes 24580
  0.0 0.7 %copy-start.7 = (f32[4]{0:T(128)S(1)}, f32[4]{0:T(128)}, u32[]{:S(2)}) copy-start(f32[4]{0:T(128)} %param.12) | copy-start | bytes 52
  0.0 0.7 %copy-start.8 = (s32[4]{0:T(128)S(1)}, s32[4]{0:T(128)}, u32[]{:S(2)}) copy-start(s32[4]{0:T(128)} %param.13) | copy-start | bytes 52
  0.7 0.8 %copy-start = (f32[8,8,256]{2,1,0:T(8,128)S(1)}, f32[8,8,256]{2,1,0:T(8,128)}, u32[]{:S(2)}) copy-start(f32[8,8,256]{2,1,0:T(8,128)} %log_conductivity.1) | copy-start | bytes 196612
  1.5 0.8 %copy-start.1 = (f32[8,8,256]{2,1,0:T(8,128)S(1)}, f32[8,8,256]{2,1,0:T(8,128)}, u32[]{:S(2)}) copy-start(f32[8,8,256]{2,1,0:T(8,128)} %storage.1) | copy-start | bytes 196612
  2.4 0.8 %copy-start.2 = (f32[8,8,256]{2,1,0:T(8,128)S(1)}, f32[8,8,256]{2,1,0:T(8,128)}, u32[]{:S(2)}) copy-start(f32[8,8,256]{2,1,0:T(8,128)} %recharge.1) | copy-start | bytes 196612
  3.2 0.8 %copy-start.3 = (f32[4,2048]{1,0:T(4,128)S(1)}, f32[4,2048]{1,0:T(4,128)}, u32[]{:S(2)}) copy-start(f32[4,2048]{1,0:T(4,128)} %observed.1) | copy-start | bytes 98308
  4.0 0.7 %copy-start.5 = (s32[2048]{0:T(1024)S(1)}, s32[2048]{0:T(1024)}, u32[]{:S(2)}) copy-start(s32[2048]{0:T(1024)} %param.16) | copy-start | bytes 24580
  4.7 0.7 %copy-start.6 = (s32[2048]{0:T(1024)S(1)}, s32[2048]{0:T(1024)}, u32[]{:S(2)}) copy-start(s32[2048]{0:T(1024)} %param.17) | copy-start | bytes 24580

commit v5 on v4

--- a/solution.py
+++ b/solution.py
@@ -126,6 +126,10 @@
         for k, (x, y, to_x, to_y, peer) in enumerate(first + second)
     ]
 
+    def middle():
+        for copy in started[len(first) :]:
+            copy.wait()
+
     def finish():
         passed = []
         for k, (x, y, to_x, to_y, peer) in enumerate(first):
@@ -134,40 +138,22 @@
             passed.append(remote(block, block, send_sems.at[6 + k], recv_sems.at[6 + k], partner))
         for copy in started[: len(first)]:
             copy.wait_send()
-        for copy in started[len(first) :] + passed:
+        for copy in passed:
             copy.wait()
 
-    return finish
-
-
-def coefficients(ext, e_ref, r_ref, alpha_ref, beta_ref, pump_cell, pump_tile):
-    def roots(x):
-        e_ref[x] = jnp.where(inside(x, 0, EXT), jnp.exp(0.5 * halves(ext, x, 0, EXT, 0)), 1.0)
-
-    rows(0, EXT, roots, 4)
-    lo, hi = 1, EXT - 1
-
-    def edge(xs, y, source_y):
-        count = xs.stop - xs.start
-        shape = (count, 8, 128)
-        first = ext[xs, source_y, 6:7, :]
-        second = ext[xs, source_y, 7:8, :]
-        logs = jnp.where(
-            iota(shape, 1) < 4, jnp.broadcast_to(first, shape), jnp.broadcast_to(second, shape)
-        )
-        gx = lax.axis_index("bx") * SIDE + xs.start - HALO + iota(shape, 0)
-        gy = lax.axis_index("by") * SIDE + y - HALO + jnp.zeros(shape, jnp.int32)
-        ok = (gx >= 0) & (gx < NX_BRICKS * SIDE) & (gy >= 0) & (gy < NY_BRICKS * SIDE)
-        e_ref[xs, y] = jnp.where(ok, jnp.exp(0.5 * logs), 1.0)
-
-    middle = slice(HALO, HALO + SIDE)
-    edge(middle, 0, 1)
-    edge(middle, EXT - 1, EXT - 2)
-    for x in (HALO - 1, HALO + SIDE):
-        edge(slice(x, x + 1), 1, 2)
-        edge(slice(x, x + 1), EXT - 2, EXT - 3)
-
-    def terms(x):
+    return middle, finish
+
+
+def roots(ext, e_ref, lo, hi):
+    def row(x):
+        logs = halves(ext, x, lo, hi, 0)
+        e_ref[x, lo:hi] = jnp.where(inside(x, lo, hi), jnp.exp(0.5 * logs), 1.0)
+
+    rows(0, EXT, row, 4)
+
+
+def terms(ext, e_ref, r_ref, alpha_ref, beta_ref, pump_cell, pump_tile, lo, hi):
+    def row(x):
         e = e_ref[x, lo:hi]
         diagonal = halves(ext, x, lo, hi, 1) + e * around(e_ref, x, lo, hi, 1.0)
         r = jnp.where(inside(x, lo, hi), 1.0 / diagonal, 0.0)
@@ -178,7 +164,29 @@
         alpha_ref[x, lo:hi] = e * er
         beta_ref[x, lo:hi] = er * source
 
-    rows(lo, hi, terms, 2)
+    rows(1, EXT - 1, row, 2)
+
+
+def edge_roots(ext, e_ref):
+    def edge(xs, y, source_y):
+        count = xs.stop - xs.start
+        shape = (count, 8, 128)
+        first = ext[xs, source_y, 6:7, :]
+        second = ext[xs, source_y, 7:8, :]
+        logs = jnp.where(
+            iota(shape, 1) < 4, jnp.broadcast_to(first, shape), jnp.broadcast_to(second, shape)
+        )
+        gx = lax.axis_index("bx") * SIDE + xs.start - HALO + iota(shape, 0)
+        gy = lax.axis_index("by") * SIDE + y - HALO + jnp.zeros(shape, jnp.int32)
+        ok = (gx >= 0) & (gx < NX_BRICKS * SIDE) & (gy >= 0) & (gy < NY_BRICKS * SIDE)
+        e_ref[xs, y] = jnp.where(ok, jnp.exp(0.5 * logs), 1.0)
+
+    middle = slice(HALO, HALO + SIDE)
+    edge(middle, 0, 1)
+    edge(middle, EXT - 1, EXT - 2)
+    for x in (HALO - 1, HALO + SIDE):
+        edge(slice(x, x + 1), 1, 2)
+        edge(slice(x, x + 1), EXT - 2, EXT - 3)
 
 
 def sweeps(e_ref, alpha_ref, beta_ref, u_ref, out_ref):
@@ -396,12 +404,23 @@
 
 
 def kernel(
-    log_conductivity, storage, recharge, owner, column, top, observed, pump_rate, pump_well, out,
+    log_hbm, storage_hbm, recharge_hbm, owner_hbm, column_hbm, top_hbm, observed_hbm,
+    pump_rate, pump_well, out,
+    log_conductivity, storage, recharge, owner, column, top, observed, load_sems,
     packed, steps_ref, lhs, ext, e_ref, r_ref, alpha_ref, heads_ref, beta_ref, u_ref, adjoint_ref, sum_ref,
     message, squares, messages, near, partial, far, parts, slots,
     halo_send, halo_recv, msg_send, msg_recv, near_send, near_recv, far_send, far_recv,
     part_send, part_recv,
 ):
+    pairs = (
+        (log_hbm, log_conductivity), (storage_hbm, storage), (recharge_hbm, recharge),
+        (owner_hbm, owner), (column_hbm, column), (top_hbm, top), (observed_hbm, observed),
+    )
+    loads = [
+        pltpu.make_async_copy(there, here, load_sems.at[i]) for i, (there, here) in enumerate(pairs)
+    ]
+    for copy in loads:
+        copy.start()
     me, bx, by = lax.axis_index("test"), lax.axis_index("bx"), lax.axis_index("by")
     turn, place = by // ROUND, lax.rem(by, ROUND)
     neighbours = [neighbour(dx, dy) for k, (dx, dy) in NEIGHBOURS]
@@ -423,14 +442,26 @@
     barrier = pltpu.get_barrier_semaphore()
     for peer in everyone:
         pl.semaphore_signal(barrier, inc=1, device_id=peer, device_id_type=MESH)
+    for copy in loads[:3]:
+        copy.wait()
     pack(log_conductivity, storage, recharge, packed)
     pl.semaphore_wait(barrier, len(everyone))
-    finish_halo = halo_copies(packed, ext, halo_send, halo_recv)
+    middle_halo, finish_halo = halo_copies(packed, ext, halo_send, halo_recv)
     ext[HALO : HALO + SIDE, HALO : HALO + SIDE] = packed[...]
+    for copy in loads[3:]:
+        copy.wait()
     pump_cell, pump_tile = pumping(pump_rate, pump_well, owner, column, top)
     wells = own_wells(owner, column, top, observed)
+    fields = (ext, e_ref, r_ref, alpha_ref, beta_ref, pump_cell, pump_tile)
+    middle_halo()
+    roots(ext, e_ref, HALO, HALO + SIDE)
+    terms(*fields, HALO + 1, HALO + SIDE - 1)
     finish_halo()
-    coefficients(ext, e_ref, r_ref, alpha_ref, beta_ref, pump_cell, pump_tile)
+    roots(ext, e_ref, 0, HALO)
+    roots(ext, e_ref, HALO + SIDE, EXT)
+    edge_roots(ext, e_ref)
+    terms(*fields, 1, HALO + 1)
+    terms(*fields, HALO + SIDE - 1, EXT - 1)
     sweeps(e_ref, alpha_ref, beta_ref, u_ref, heads_ref)
     residuals(heads_ref, wells, message, squares)
     near_copies = [
@@ -498,16 +529,20 @@
     return pl.pallas_call(
         kernel,
         out_shape=jax.ShapeDtypeStruct((SIDE, SIDE, 32), F32),
-        in_specs=[pl.BlockSpec(memory_space=VMEM)] * 9,
+        in_specs=[pl.BlockSpec(memory_space=pltpu.HBM)] * 7
+        + [pl.BlockSpec(memory_space=VMEM)] * 2,
         out_specs=pl.BlockSpec(memory_space=VMEM),
-        scratch_shapes=[
+        scratch_shapes=[VMEM((SIDE, SIDE, 256), F32)] * 3
+        + [VMEM((16, 128), jnp.int32)] * 3
+        + [VMEM((4, WELLS), F32), dma((7,))]
+        + [
             VMEM((SIDE, SIDE) + tile, F32),
             VMEM((6, SIDE, SIDE) + tile, F32),
             VMEM((EXT - 2, (EXT - 2) * 8, GROUPS * 128), jnp.bfloat16),
         ]
         + [VMEM(s, F32) for s in scratch] + [dma((n,)) for n in counts],
         compiler_params=pltpu.CompilerParams(
-            vmem_limit_bytes=48 * 1024 * 1024, collective_id=0, has_side_effects=True
+            vmem_limit_bytes=67_043_328, collective_id=0, has_side_effects=True
         ),
     )(
         log_conductivity, storage, recharge, *table, observed,

time: 55.9 us -> 52.3 us (0.936)
  local copies, waits for them, and re-layouts: 5.98 us -> 1.38 us
  Pallas kernels: 49.4 us -> 50.7 us
    unnamed x19 -> x1, local copies, waits for them, and re-layouts: 5.98 us -> 1.38 us
    pallas_call x1, Pallas kernels: 49.4 us -> 50.7 us  [local(): pl.pallas_call(kernel, out_shape=jax.ShapeDtypeStruct((SIDE, SIDE, 32), F...]
where the time goes in v5:
time: 52.3 us; the launch traced here: 52.1 us
  Pallas kernels  50.7 us (97%)
  local copies, waits for them, and re-layouts  1.38 us (3%)
    pallas_call x1, Pallas kernels, local(): pl.pallas_call(kernel, out_shape=jax.ShapeDtypeStruct((SIDE, SIDE, 32), F...  50.7 us
    unnamed x1, local copies, waits for them, and re-layouts  1.38 us

profile of v5, /device:TPU:1, one launch (start us, length us, event | category | flops | bytes accessed | tf_op | source)
XLA Modules:
  0.0 52.1 jit_solution(8433525135755189891)
XLA Ops:
  0.0 50.7 %shard_map.91 = f32[8,8,32]{2,1,0:T(8,128)} custom-call(f32[8,8,256]{2,1,0:T(8,128)} %log_hbm.1, f32[8,8,256]{2,1,0:T(8,128)} %storage_hbm.1, f32[8,8,256]{2,1,0:T(8,128)} %recharge_hbm.1, s32[16,128]{1,0:T(8,128)} %bitcast.5, s32[16,128]{1,0:T(8,128)} %bitcast.6, s32[16,128]{1,0:T(8,128)} %bitcast.7, f32[4,2048]{1,0:T(4,128)} %observed_hbm.1, ...), custom_call_target="tpu_custom_call" | custom-call | tf_op jit(solution)/shard_map/pallas_call | solution.py:529
  50.7 1.4 %copy.11 = f32[8,8,32]{2,1,0:T(8,128)} copy(f32[8,8,32]{2,1,0:T(8,128)} %shard_map.91) | data formatting | bytes 16384

commit v6 on v5

--- a/solution.py
+++ b/solution.py
@@ -101,58 +101,69 @@
     me = lax.axis_index("test")
     core = lax.rem(me, 2)
     partner = {"test": me + 1 - 2 * core}
-    deep = HALO - 1
-    first, second = [], []
     half = pl.ds(SIDE // 2 * core, SIDE // 2)
     half_there = pl.ds(HALO + SIDE // 2 * core, SIDE // 2)
-    corner = pl.ds((SIDE - deep) * core, deep)
-    corner_there = pl.ds((HALO + SIDE) * (1 - core) + core, deep)
-    for dy, from_y, to_y, skip in ((1, SIDE - deep, 1, 1), (-1, 0, HALO + SIDE, 0)):
-        first.append(
-            (half, pl.ds(from_y, deep), half_there, pl.ds(to_y, deep), neighbour(0, dy))
-        )
-        first.append(
-            (corner, pl.ds(from_y + skip, deep - 1), corner_there, pl.ds(to_y + skip, deep - 1),
-             neighbour(2 * core - 1, dy))
-        )
-    first = [first[0], first[2], first[1], first[3]]
-    for dx, from_x, to_x in ((1, SIDE - HALO, 0), (-1, 0, HALO + SIDE)):
-        second.append(
-            (pl.ds(from_x, HALO), pl.ds(0, SIDE), pl.ds(to_x, HALO), pl.ds(HALO, SIDE),
-             neighbour(dx, 0))
-        )
+
+    def along_x(near, far):
+        count = far - near + 1
+        here = (near - 1) * (1 - core) + (SIDE - far) * core
+        there = (HALO + SIDE + near - 1) * (1 - core) + (HALO - far) * core
+        return pl.ds(here, count), pl.ds(there, count)
+
+    def along_y(dy, near, far):
+        count = far - near + 1
+        if dy > 0:
+            return pl.ds(SIDE - far, count), pl.ds(HALO - far, count)
+        return pl.ds(near - 1, count), pl.ds(HALO + SIDE + near - 1, count)
+
+    def block(xs, dy, near, far, dx):
+        ys = along_y(dy, near, far)
+        return xs[0], ys[0], xs[1], ys[1], neighbour(dx, dy)
+
+    face, side = (half, half_there), 2 * core - 1
+    near = [block(face, dy, 1, 2, 0) for dy in (1, -1)]
+    near += [block(along_x(1, 2), dy, 1, 1, side) for dy in (1, -1)]
+    outer = [block(face, dy, 3, 3, 0) for dy in (1, -1)]
+    outer += [block(along_x(1, 3), dy, 2, 2, side) for dy in (1, -1)]
+    outer += [block(along_x(3, 3), dy, 1, 1, side) for dy in (1, -1)]
+    across = [
+        (pl.ds(from_x, HALO), pl.ds(0, SIDE), pl.ds(to_x, HALO), pl.ds(HALO, SIDE), neighbour(dx, 0))
+        for dx, from_x, to_x in ((1, SIDE - HALO, 0), (-1, 0, HALO + SIDE))
+    ]
+    plan = near + across + outer
     started = [
         remote(packed.at[x, y], ext.at[to_x, to_y], send_sems.at[k], recv_sems.at[k], peer)
-        for k, (x, y, to_x, to_y, peer) in enumerate(first + second)
+        for k, (x, y, to_x, to_y, peer) in enumerate(plan)
     ]
 
     def middle():
-        for copy in started[len(first) :]:
+        for copy in started[4:6]:
             copy.wait()
 
-    def finish():
+    def finish(lo, hi):
         passed = []
-        for k, (x, y, to_x, to_y, peer) in enumerate(first):
+        for k in range(lo, hi):
+            x, y, to_x, to_y, peer = plan[k]
             started[k].wait_recv()
             block = ext.at[to_x, to_y]
-            passed.append(remote(block, block, send_sems.at[6 + k], recv_sems.at[6 + k], partner))
-        for copy in started[: len(first)]:
+            passed.append(remote(block, block, send_sems.at[12 + k], recv_sems.at[12 + k], partner))
+        for copy in started[lo:hi]:
             copy.wait_send()
         for copy in passed:
             copy.wait()
 
-    return middle, finish
-
-
-def roots(ext, e_ref, lo, hi):
+    return middle, lambda: finish(0, 4), lambda: finish(6, 12)
+
+
+def roots(ext, e_ref, lo, hi, first=0, last=EXT, group=4):
     def row(x):
         logs = halves(ext, x, lo, hi, 0)
         e_ref[x, lo:hi] = jnp.where(inside(x, lo, hi), jnp.exp(0.5 * logs), 1.0)
 
-    rows(0, EXT, row, 4)
-
-
-def terms(ext, e_ref, r_ref, alpha_ref, beta_ref, pump_cell, pump_tile, lo, hi):
+    rows(first, last, row, group)
+
+
+def terms(ext, e_ref, r_ref, alpha_ref, beta_ref, pump_cell, pump_tile, lo, hi, first=1, last=EXT - 1):
     def row(x):
         e = e_ref[x, lo:hi]
         diagonal = halves(ext, x, lo, hi, 1) + e * around(e_ref, x, lo, hi, 1.0)
@@ -164,44 +175,67 @@
         alpha_ref[x, lo:hi] = e * er
         beta_ref[x, lo:hi] = er * source
 
-    rows(1, EXT - 1, row, 2)
+    rows(first, last, row, 2)
+
+
+def edge(ext, e_ref, xs, y, source_y):
+    count = xs.stop - xs.start
+    shape = (count, 8, 128)
+    first = ext[xs, source_y, 6:7, :]
+    second = ext[xs, source_y, 7:8, :]
+    logs = jnp.where(
+        iota(shape, 1) < 4, jnp.broadcast_to(first, shape), jnp.broadcast_to(second, shape)
+    )
+    gx = lax.axis_index("bx") * SIDE + xs.start - HALO + iota(shape, 0)
+    gy = lax.axis_index("by") * SIDE + y - HALO + jnp.zeros(shape, jnp.int32)
+    ok = (gx >= 0) & (gx < NX_BRICKS * SIDE) & (gy >= 0) & (gy < NY_BRICKS * SIDE)
+    e_ref[xs, y] = jnp.where(ok, jnp.exp(0.5 * logs), 1.0)
+
+
+MIDDLE = slice(HALO, HALO + SIDE)
 
 
 def edge_roots(ext, e_ref):
-    def edge(xs, y, source_y):
-        count = xs.stop - xs.start
-        shape = (count, 8, 128)
-        first = ext[xs, source_y, 6:7, :]
-        second = ext[xs, source_y, 7:8, :]
-        logs = jnp.where(
-            iota(shape, 1) < 4, jnp.broadcast_to(first, shape), jnp.broadcast_to(second, shape)
-        )
-        gx = lax.axis_index("bx") * SIDE + xs.start - HALO + iota(shape, 0)
-        gy = lax.axis_index("by") * SIDE + y - HALO + jnp.zeros(shape, jnp.int32)
-        ok = (gx >= 0) & (gx < NX_BRICKS * SIDE) & (gy >= 0) & (gy < NY_BRICKS * SIDE)
-        e_ref[xs, y] = jnp.where(ok, jnp.exp(0.5 * logs), 1.0)
-
-    middle = slice(HALO, HALO + SIDE)
-    edge(middle, 0, 1)
-    edge(middle, EXT - 1, EXT - 2)
+    edge(ext, e_ref, MIDDLE, 0, 1)
+    edge(ext, e_ref, MIDDLE, EXT - 1, EXT - 2)
     for x in (HALO - 1, HALO + SIDE):
-        edge(slice(x, x + 1), 1, 2)
-        edge(slice(x, x + 1), EXT - 2, EXT - 3)
-
-
-def sweeps(e_ref, alpha_ref, beta_ref, u_ref, out_ref):
+        edge(ext, e_ref, slice(x, x + 1), 1, 2)
+        edge(ext, e_ref, slice(x, x + 1), EXT - 2, EXT - 3)
+
+
+def near_coefficients(fields):
+    ext, e_ref = fields[:2]
+    lo, hi = HALO, HALO + SIDE
+    for first, last in ((lo - 2, lo), (hi, hi + 2)):
+        roots(ext, e_ref, first, last, lo, hi)
+        for column in (lo - 1, hi):
+            roots(ext, e_ref, column, column + 1, first, last, 2)
+    edge(ext, e_ref, MIDDLE, lo - 3, lo - 2)
+    edge(ext, e_ref, MIDDLE, hi + 2, hi + 1)
+    for x in (lo - 1, hi):
+        edge(ext, e_ref, slice(x, x + 1), lo - 2, lo - 1)
+        edge(ext, e_ref, slice(x, x + 1), hi + 1, hi)
+    terms(*fields, lo - 2, lo + 1, lo, hi)
+    terms(*fields, hi - 1, hi + 2, lo, hi)
+    for first in (lo - 2, hi):
+        terms(*fields, lo - 1, lo + 1, first, first + 2)
+        terms(*fields, hi - 1, hi + 1, first, first + 2)
+
+
+def sweeps(e_ref, alpha_ref, beta_ref, u_ref, out_ref, first):
     def second(x):
-        u_ref[x, 2 : EXT - 2] = beta_ref[x, 2 : EXT - 2] + alpha_ref[x, 2 : EXT - 2] * around(
-            beta_ref, x, 2, EXT - 2, 0.0
-        )
-
-    rows(2, EXT - 2, second, 4)
+        u_ref[x, first : EXT - first] = beta_ref[x, first : EXT - first] + alpha_ref[
+            x, first : EXT - first
+        ] * around(beta_ref, x, first, EXT - first, 0.0)
+
+    rows(first, EXT - first, second, 2)
+    lo, hi = first + 1, EXT - first - 1
 
     def third(x):
-        u = beta_ref[x, 3 : EXT - 3] + alpha_ref[x, 3 : EXT - 3] * around(u_ref, x, 3, EXT - 3, 0.0)
-        out_ref[x, 3 : EXT - 3] = u / e_ref[x, 3 : EXT - 3]
-
-    rows(3, EXT - 3, third, 5)
+        u = beta_ref[x, lo:hi] + alpha_ref[x, lo:hi] * around(u_ref, x, lo, hi, 0.0)
+        out_ref[x, lo:hi] = u / e_ref[x, lo:hi]
+
+    rows(lo, hi, third, 2)
 
 
 def pumping(pump_rate, pump_well, owner, column, top):
@@ -446,7 +480,7 @@
         copy.wait()
     pack(log_conductivity, storage, recharge, packed)
     pl.semaphore_wait(barrier, len(everyone))
-    middle_halo, finish_halo = halo_copies(packed, ext, halo_send, halo_recv)
+    middle_halo, near_halo, outer_halo = halo_copies(packed, ext, halo_send, halo_recv)
     ext[HALO : HALO + SIDE, HALO : HALO + SIDE] = packed[...]
     for copy in loads[3:]:
         copy.wait()
@@ -456,23 +490,26 @@
     middle_halo()
     roots(ext, e_ref, HALO, HALO + SIDE)
     terms(*fields, HALO + 1, HALO + SIDE - 1)
-    finish_halo()
+    near_halo()
+    near_coefficients(fields)
+    sweeps(e_ref, alpha_ref, beta_ref, u_ref, heads_ref, 3)
+    residuals(heads_ref, wells, message, squares)
+    near_copies = [
+        remote(squares, near.at[i], near_send.at[i], near_recv.at[i], peer)
+        for i, peer in enumerate(near_peers)
+    ]
+    copies = [
+        remote(message, messages.at[8 - k], msg_send.at[k], msg_recv.at[k], neighbour(dx, dy))
+        for k, (dx, dy) in NEIGHBOURS
+    ]
+    messages[4] = message[...]
+    outer_halo()
     roots(ext, e_ref, 0, HALO)
     roots(ext, e_ref, HALO + SIDE, EXT)
     edge_roots(ext, e_ref)
     terms(*fields, 1, HALO + 1)
     terms(*fields, HALO + SIDE - 1, EXT - 1)
-    sweeps(e_ref, alpha_ref, beta_ref, u_ref, heads_ref)
-    residuals(heads_ref, wells, message, squares)
-    near_copies = [
-        remote(squares, near.at[i], near_send.at[i], near_recv.at[i], peer)
-        for i, peer in enumerate(near_peers)
-    ]
-    copies = [
-        remote(message, messages.at[8 - k], msg_send.at[k], msg_recv.at[k], neighbour(dx, dy))
-        for k, (dx, dy) in NEIGHBOURS
-    ]
-    messages[4] = message[...]
+    sweeps(e_ref, alpha_ref, beta_ref, u_ref, heads_ref, 2)
     for copy in near_copies:
         copy.wait()
     here = squares[...]
@@ -487,7 +524,7 @@
     for copy in copies:
         copy.wait()
     adjoint_source(messages, e_ref, r_ref, beta_ref, lhs)
-    sweeps(e_ref, alpha_ref, beta_ref, u_ref, adjoint_ref)
+    sweeps(e_ref, alpha_ref, beta_ref, u_ref, adjoint_ref, 2)
     for copy in far_copies:
         copy.wait()
     total = partial[...]
@@ -525,7 +562,7 @@
         (SIDE, SIDE) + tile, tile, tile, (9,) + tile,
         (near,) + tile, tile, (far,) + tile, (TESTS_AXIS, 2) + tile, (TESTS_AXIS - 1, 2) + tile,
     ]
-    counts = (10, 10, 9, 9, near, near, far, far, TESTS_AXIS - 1, TESTS_AXIS - 1)
+    counts = (24, 24, 9, 9, near, near, far, far, TESTS_AXIS - 1, TESTS_AXIS - 1)
     return pl.pallas_call(
         kernel,
         out_shape=jax.ShapeDtypeStruct((SIDE, SIDE, 32), F32),

time: 52.3 us -> 51.6 us (0.987)
  Pallas kernels: 50.7 us -> 50 us
    pallas_call x1, Pallas kernels: 50.7 us -> 50 us  [local(): pl.pallas_call(kernel, out_shape=jax.ShapeDtypeStruct((SIDE, SIDE, 32), F...]
where the time goes in v6:
time: 51.6 us; the launch traced here: 51.4 us
  Pallas kernels  50 us (97%)
  local copies, waits for them, and re-layouts  1.38 us (3%)
    pallas_call x1, Pallas kernels, local(): pl.pallas_call(kernel, out_shape=jax.ShapeDtypeStruct((SIDE, SIDE, 32), F...  50 us
    unnamed x1, local copies, waits for them, and re-layouts  1.38 us

profile of v6, /device:TPU:1, one launch (start us, length us, event | category | flops | bytes accessed | tf_op | source)
XLA Modules:
  0.0 51.4 jit_solution(13303612829134673703)
XLA Ops:
  0.0 50.0 %shard_map.91 = f32[8,8,32]{2,1,0:T(8,128)} custom-call(f32[8,8,256]{2,1,0:T(8,128)} %log_hbm.1, f32[8,8,256]{2,1,0:T(8,128)} %storage_hbm.1, f32[8,8,256]{2,1,0:T(8,128)} %recharge_hbm.1, s32[16,128]{1,0:T(8,128)} %bitcast.5, s32[16,128]{1,0:T(8,128)} %bitcast.6, s32[16,128]{1,0:T(8,128)} %bitcast.7, f32[4,2048]{1,0:T(4,128)} %observed_hbm.1, ...), custom_call_target="tpu_custom_call" | custom-call | tf_op jit(solution)/shard_map/pallas_call | solution.py:566
  50.0 1.4 %copy.11 = f32[8,8,32]{2,1,0:T(8,128)} copy(f32[8,8,32]{2,1,0:T(8,128)} %shard_map.91) | data formatting | bytes 16384

commit v7 on v6

--- a/solution.py
+++ b/solution.py
@@ -228,14 +228,14 @@
             x, first : EXT - first
         ] * around(beta_ref, x, first, EXT - first, 0.0)
 
-    rows(first, EXT - first, second, 2)
+    rows(first, EXT - first, second, 4 if (EXT - 2 * first) % 4 == 0 else 5)
     lo, hi = first + 1, EXT - first - 1
 
     def third(x):
         u = beta_ref[x, lo:hi] + alpha_ref[x, lo:hi] * around(u_ref, x, lo, hi, 0.0)
         out_ref[x, lo:hi] = u / e_ref[x, lo:hi]
 
-    rows(lo, hi, third, 2)
+    rows(lo, hi, third, 4 if (hi - lo) % 4 == 0 else 5)
 
 
 def pumping(pump_rate, pump_well, owner, column, top):
@@ -402,7 +402,7 @@
     rows(lo, hi, row, 2)
 
 
-def sensitivity(steps_ref, adjoint_ref, scale, out_ref):
+def sensitivity(steps_ref, adjoint_ref, out_ref):
     lo, hi = HALO, HALO + SIDE
 
     def row(x):
@@ -414,11 +414,18 @@
             )
         for f, a_n in enumerate(z_neighbours(a, 0.0)):
             total = total + steps_ref[4 + f, x - HALO] * (a - a_n)
-        total = total * scale[None]
+        out_ref[x - HALO] = total
+
+    rows(lo, hi, row, 4)
+
+
+def sum_tests(sum_ref, scale):
+    def row(x):
+        total = sum_ref[x] * scale[None]
         total = total + pltpu.roll(total, 7, 1)
-        out_ref[x - HALO] = total + pltpu.roll(total, 6, 1)
-
-    rows(lo, hi, row, 4)
+        sum_ref[x] = total + pltpu.roll(total, 6, 1)
+
+    rows(0, SIDE, row, 4)
 
 
 def slabs(sum_ref, out):
@@ -509,7 +516,6 @@
     edge_roots(ext, e_ref)
     terms(*fields, 1, HALO + 1)
     terms(*fields, HALO + SIDE - 1, EXT - 1)
-    sweeps(e_ref, alpha_ref, beta_ref, u_ref, heads_ref, 2)
     for copy in near_copies:
         copy.wait()
     here = squares[...]
@@ -520,18 +526,20 @@
         remote(partial, far.at[i], far_send.at[i], far_recv.at[i], peer)
         for i, peer in enumerate(far_peers)
     ]
+    sweeps(e_ref, alpha_ref, beta_ref, u_ref, heads_ref, 2)
     head_steps(e_ref, heads_ref, steps_ref)
     for copy in copies:
         copy.wait()
     adjoint_source(messages, e_ref, r_ref, beta_ref, lhs)
     sweeps(e_ref, alpha_ref, beta_ref, u_ref, adjoint_ref, 2)
+    sensitivity(steps_ref, adjoint_ref, sum_ref)
     for copy in far_copies:
         copy.wait()
     total = partial[...]
     for i in range(len(far_peers)):
         total = total + far[i]
-    scale = (-0.5 / (4 * TESTS_AXIS)) / (total / WELLS + EPSILON)
-    sensitivity(steps_ref, adjoint_ref, scale, sum_ref)
+    scale = 1.0 / (total / WELLS + EPSILON)
+    sum_tests(sum_ref, scale)
     slabs(sum_ref, parts)
     part_copies = [
         remote(parts.at[peer], slots.at[i], part_send.at[i], part_recv.at[i], {"test": peer})
@@ -563,7 +571,7 @@
         (near,) + tile, tile, (far,) + tile, (TESTS_AXIS, 2) + tile, (TESTS_AXIS - 1, 2) + tile,
     ]
     counts = (24, 24, 9, 9, near, near, far, far, TESTS_AXIS - 1, TESTS_AXIS - 1)
-    return pl.pallas_call(
+    total = pl.pallas_call(
         kernel,
         out_shape=jax.ShapeDtypeStruct((SIDE, SIDE, 32), F32),
         in_specs=[pl.BlockSpec(memory_space=pltpu.HBM)] * 7
@@ -585,6 +593,7 @@
         log_conductivity, storage, recharge, *table, observed,
         pump_rate.reshape(1, 4), pump_well.reshape(1, 4),
     )
+    return total * (-0.5 / (4 * TESTS_AXIS))
 
 
 def solution(mesh):

time: 51.6 us -> 50.8 us (0.984)
  other arithmetic: 0 us -> 1.38 us
  local copies, waits for them, and re-layouts: 1.38 us -> 0 us
  Pallas kernels: 50 us -> 49.2 us
    mul x0 -> x1, other arithmetic: none -> 1.38 us  [local(): return total * (-0.5 / (4 * TESTS_AXIS))]
    unnamed x1 -> x0, local copies, waits for them, and re-layouts: 1.38 us -> none
    pallas_call x1, Pallas kernels: 50 us -> 49.2 us  [local(): pl.pallas_call(kernel, out_shape=jax.ShapeDtypeStruct((SIDE, SIDE, 32), F...]
where the time goes in v7:
time: 50.8 us; the launch traced here: 50.6 us
  Pallas kernels  49.2 us (97%)
  other arithmetic  1.38 us (3%)
    pallas_call x1, Pallas kernels, local(): pl.pallas_call(kernel, out_shape=jax.ShapeDtypeStruct((SIDE, SIDE, 32), F...  49.2 us
    mul x1, other arithmetic, local(): return total * (-0.5 / (4 * TESTS_AXIS))  1.38 us

profile of v7, /device:TPU:1, one launch (start us, length us, event | category | flops | bytes accessed | tf_op | source)
XLA Modules:
  0.0 50.6 jit_solution(815197859130055432)
XLA Ops:
  0.0 49.2 %shard_map.91 = f32[8,8,32]{2,1,0:T(8,128)} custom-call(f32[8,8,256]{2,1,0:T(8,128)} %log_hbm.1, f32[8,8,256]{2,1,0:T(8,128)} %storage_hbm.1, f32[8,8,256]{2,1,0:T(8,128)} %recharge_hbm.1, s32[16,128]{1,0:T(8,128)} %bitcast.5, s32[16,128]{1,0:T(8,128)} %bitcast.6, s32[16,128]{1,0:T(8,128)} %bitcast.7, f32[4,2048]{1,0:T(4,128)} %observed_hbm.1, ...), custom_call_target="tpu_custom_call" | custom-call | tf_op jit(solution)/shard_map/pallas_call | solution.py:574
  49.2 1.4 %broadcast_multiply_fusion = f32[8,8,32]{2,1,0:T(8,128)} fusion(f32[8,8,32]{2,1,0:T(8,128)} %shard_map.91), kind=kLoop, calls=%fused_computation | loop fusion | flops 2048 | bytes 16384 | tf_op jit(solution)/shard_map/mul | solution.py:596

commit v8 on v7

--- a/solution.py
+++ b/solution.py
@@ -175,7 +175,8 @@
         alpha_ref[x, lo:hi] = e * er
         beta_ref[x, lo:hi] = er * source
 
-    rows(first, last, row, 2)
+    count = last - first
+    rows(first, last, row, 7 if count % 7 == 0 else min(count, 4))
 
 
 def edge(ext, e_ref, xs, y, source_y):
@@ -374,7 +375,7 @@
                 .astype(jnp.bfloat16)
             )
 
-    rows(lo, hi, left, 2)
+    rows(lo, hi, left, 7)
     group = 7
     for first in range(0, wide, group):
         block = lhs[first : first + group].reshape(group * wide * 8, GROUPS * 128)

time: 50.8 us -> 50.5 us (level)
  no operation moved by 1% of the time
where the time goes in v8:
time: 50.5 us; the launch traced here: 50.2 us
  Pallas kernels  48.9 us (97%)
  other arithmetic  1.38 us (3%)
    pallas_call x1, Pallas kernels, local(): pl.pallas_call(kernel, out_shape=jax.ShapeDtypeStruct((SIDE, SIDE, 32), F...  48.9 us
    mul x1, other arithmetic, local(): return total * (-0.5 / (4 * TESTS_AXIS))  1.38 us

profile of v8, /device:TPU:1, one launch (start us, length us, event | category | flops | bytes accessed | tf_op | source)
XLA Modules:
  0.0 50.2 jit_solution(16916816869303242798)
XLA Ops:
  0.0 48.9 %shard_map.91 = f32[8,8,32]{2,1,0:T(8,128)} custom-call(f32[8,8,256]{2,1,0:T(8,128)} %log_hbm.1, f32[8,8,256]{2,1,0:T(8,128)} %storage_hbm.1, f32[8,8,256]{2,1,0:T(8,128)} %recharge_hbm.1, s32[16,128]{1,0:T(8,128)} %bitcast.5, s32[16,128]{1,0:T(8,128)} %bitcast.6, s32[16,128]{1,0:T(8,128)} %bitcast.7, f32[4,2048]{1,0:T(4,128)} %observed_hbm.1, ...), custom_call_target="tpu_custom_call" | custom-call | tf_op jit(solution)/shard_map/pallas_call | solution.py:575
  48.9 1.4 %broadcast_multiply_fusion = f32[8,8,32]{2,1,0:T(8,128)} fusion(f32[8,8,32]{2,1,0:T(8,128)} %shard_map.91), kind=kLoop, calls=%fused_computation | loop fusion | flops 2048 | bytes 16384 | tf_op jit(solution)/shard_map/mul | solution.py:597
